TPU v7x, 32 devices: a whole 2x2x4 slice. The times are simulated.
32 devices in a mesh: groups: 2 (over x), row: 16 (over z, y, core).
Axes of the slice: x: 2, y: 2, z: 4, core: 2. Of those that a mesh axis runs over, the one named last changes fastest.
Arguments:
- forces: bfloat16 [2048, 768], P(('groups', 'row')), parts along dimension 0, may hold values from -6 to 6
- tiles: bfloat16 [32768, 96, 96], P(('groups', 'row')), parts along dimension 0, may hold values from -0.109375 to 0.109375
- tile_local: int32 [32768], P(('groups', 'row')), parts along dimension 0, may hold values from 0 to 63
- tile_slot: int32 [32768], P(('groups', 'row')), parts along dimension 0, may hold values from 0 to 255
- tile_flag: int32 [32768], P(('groups', 'row')), parts along dimension 0, may hold values 0 or 1
- want_list: int32 [32, 16, 16], P(('groups', 'row')), parts along dimension 0, may hold values from 0 to 63
Outputs:
- krylov_one: bfloat16 [2048, 768], P(('groups', 'row')), parts along dimension 0
- krylov_two: bfloat16 [2048, 768], P(('groups', 'row')), parts along dimension 0
There are 2 independent parts, one for each index of `groups`. A program takes and returns all parts, laid end to end along the dimension named above; each array names one. Nothing has to cross between parts.
All inputs are finite; a program needn't handle non-finite values. No bound on the sum of `tile_flag` on one device may be relied on, other than what follows from the above.
Results may differ from a plain program's by a relative error of at most 0.0041.
Values may be sent and summed in bfloat16 or wider, within the bound.
No kernel may reach another device: no remote copies, remote signals or barrier semaphores. Data moves between devices by JAX's collectives and lax.ppermute only.
A program may use at most 128 MiB of HBM per device.

v0:
```python
import jax
import jax.numpy as jnp
from jax import lax
from jax.sharding import PartitionSpec as P

NRHS = 8


def one_hot_table(index, count, kind):
    return (index[:, None] == jnp.arange(count, dtype=jnp.int32)[None, :]).astype(kind)


def pick_rows(table, values):
    return jnp.dot(table, values, preferred_element_type=jnp.float32).astype(jnp.bfloat16)


def sum_rows(table, partial_rows):
    return lax.dot_general(
        table,
        partial_rows,
        (((0,), (0,)), ((), ())),
        precision=lax.Precision.HIGHEST,
        preferred_element_type=jnp.float32,
    )


def per_device(forces, tiles, tile_local, tile_slot, tile_flag, want_list):
    peer_count = lax.axis_size("row")
    fibres = forces.shape[0]
    row_width = forces.shape[1]
    unknowns = tiles.shape[1]
    capacity = want_list.shape[2]
    blocks = tiles.shape[0]
    slot_total = peer_count * capacity
    wanted = want_list[0]
    mirror_gate = tile_flag.astype(jnp.float32)[:, None, None]
    local_pick = one_hot_table(tile_local, fibres, jnp.bfloat16)
    local_sum = one_hot_table(tile_local, fibres, jnp.float32)
    slot_pick = one_hot_table(tile_slot, slot_total, jnp.bfloat16)
    slot_sum = one_hot_table(tile_slot, slot_total, jnp.float32)
    global_rows = (jnp.arange(peer_count, dtype=jnp.int32)[:, None] * fibres + wanted).reshape(-1)
    global_pick = one_hot_table(global_rows, fibres * peer_count, jnp.bfloat16)
    global_sum = one_hot_table(global_rows, fibres * peer_count, jnp.float32)

    def operate(current):
        own_forces = pick_rows(local_pick, current).reshape(blocks, NRHS, unknowns)
        mirror = (
            jnp.einsum("kij,kri->krj", tiles, own_forces, preferred_element_type=jnp.float32)
            * mirror_gate
        )
        slot_part = sum_rows(slot_sum, mirror.reshape(blocks, row_width))
        all_rows = lax.all_gather(current, "row", axis=0, tiled=True)
        slot_forces = pick_rows(global_pick, all_rows)
        far_forces = pick_rows(slot_pick, slot_forces).reshape(blocks, NRHS, unknowns)
        direct = jnp.einsum("kij,krj->kri", tiles, far_forces, preferred_element_type=jnp.float32)
        own_part = sum_rows(local_sum, direct.reshape(blocks, row_width))
        dense_part = sum_rows(global_sum, slot_part)
        returned = lax.psum_scatter(dense_part, "row", scatter_dimension=0, tiled=True)
        return (own_part + returned).astype(jnp.bfloat16)

    krylov_one = operate(forces)
    krylov_two = operate(krylov_one)
    return (krylov_one, krylov_two)


def solution(mesh):
    in_specs = (
        P(("groups", "row"), None),
        P(("groups", "row"), None, None),
        P(("groups", "row")),
        P(("groups", "row")),
        P(("groups", "row")),
        P(("groups", "row"), None, None),
    )
    out_specs = (P(("groups", "row"), None), P(("groups", "row"), None))
    return jax.shard_map(
        per_device, mesh=mesh, in_specs=in_specs, out_specs=out_specs, check_vma=False
    )
```

profile of v0, /device:TPU:0, one launch (start us, length us, event | category | flops | bytes accessed | tf_op | source)
XLA Modules:
  0.0 256.3 jit_solution(7490937594834433806)
XLA Ops:
  7.2 0.7 all-gather.3.cloned.1.call-update
  8.0 29.6 %copy.17 = bf16[1024,96,96]{2,1,0:T(8,128)(2,1)} copy(bf16[1024,96,96]{0,2,1:T(8,128)(2,1)} %param.7) | data formatting | bytes 37748736 | tf_op args[1]
  37.6 1.9 convolution_convert_fusion.1
  39.5 3.3 %copy.19 = bf16[1024,8,96]{2,1,0:T(8,128)(2,1)S(1)} copy(bf16[1024,8,96]{0,2,1:T(8,128)(2,1)} %bitcast.30) | data formatting | bytes 3145728 | tf_op jit(solution)/shard_map/reshape | solution.py:46
  42.8 13.6 %broadcast_multiply_fusion.1 = f32[1024,8,96]{2,1,0:T(8,128)} fusion(f32[1024]{0:T(1024)S(1)} %convert_element_type.36, bf16[1024,8,96]{2,1,0:T(8,128)(2,1)S(1)} %copy.19, bf16[1024,96,96]{2,1,0:T(8,128)(2,1)} %copy.17), kind=kOutput, calls=%fused_computation.1 | convolution fusion | flops 151781376 | bytes 23597056 | tf_op jit(solution)/shard_map/kij,kri->krj/dot_general | solution.py:48
  56.4 3.9 %copy.21 = f32[1024,8,96]{0,2,1:T(8,128)S(1)} copy(f32[1024,8,96]{2,1,0:T(8,128)} %broadcast_multiply_fusion.1) | data formatting | bytes 6291456 | tf_op jit(solution)/shard_map/mul | solution.py:48
  60.3 0.1 add.24
  60.4 0.1 add.25
  60.4 0.1 squeeze.3
  60.5 2.0 fusion.7
  62.6 3.4 %fusion.3 = f32[1024,768]{1,0:T(8,128)} fusion(f32[256,768]{1,0:T(8,128)S(1)} %fusion.7, s32[256]{0:T(256)S(1)} %add.26), kind=kOutput, calls=%fused_computation.14 | convolution fusion | flops 2416181248 | bytes 3933184 | tf_op jit(solution)/shard_map/dot_general | solution.py:18
  66.0 0.2 all-gather.5.cloned.1.call-start
  66.2 4.0 %convolution_convert_fusion.3 = bf16[1024,768]{0,1:T(8,128)(2,1)} fusion(bf16[1024,768]{1,0:T(8,128)(2,1)} %all-gather.3.cloned.1.call-done, s32[256]{0:T(256)S(1)} %add.26, s32[1024]{0:T(1024)S(1)} %copy-done.2), kind=kOutput, calls=%fused_computation.5 | convolution fusion | flops 806813696 | bytes 3150848 | tf_op jit(solution)/shard_map/dot_general | solution.py:14
  70.3 3.3 %copy.16 = bf16[1024,8,96]{2,1,0:T(8,128)(2,1)S(1)} copy(bf16[1024,8,96]{0,2,1:T(8,128)(2,1)} %bitcast.33) | data formatting | bytes 3145728 | tf_op jit(solution)/shard_map/reshape | solution.py:54
  73.5 18.1 %fusion.26 = f32[1024,8,96]{2,1,0:T(8,128)} fusion(bf16[1024,8,96]{2,1,0:T(8,128)(2,1)S(1)} %copy.16, bf16[1024,96,96]{2,1,0:T(8,128)(2,1)} %copy.17), kind=kOutput, calls=%fused_computation.34 | convolution fusion | flops 150994944 | bytes 23592960 | tf_op jit(solution)/shard_map/kij,krj->kri/dot_general | solution.py:55
  91.6 3.9 %copy.18 = f32[1024,8,96]{0,2,1:T(8,128)S(1)} copy(f32[1024,8,96]{2,1,0:T(8,128)} %fusion.26) | data formatting | bytes 6291456 | tf_op jit(solution)/shard_map/kij,krj->kri/dot_general | solution.py:55
  95.5 39.6 %reduce-scatter.3.cloned.1.call-done = f32[64,768]{1,0:T(8,128)} async-done(((f32[1024,768]{1,0:T(8,128)}), f32[64,768]{1,0:T(8,128)}) %reduce-scatter.3.cloned.1.call-update) | async-done | bytes 196624 | tf_op jit(solution)/shard_map/reduce_scatter | solution.py:58
  135.1 3.5 %fusion = bf16[64,768]{1,0:T(8,128)(2,1)} fusion(f32[64,768]{1,0:T(8,128)} %reduce-scatter.3.cloned.1.call-done, f32[1024,768]{0,1:T(8,128)S(1)} %bitcast.28, s32[1024]{0:T(1024)S(1)} %copy-done.1), kind=kOutput, calls=%fused_computation.10 | convolution fusion | flops 604209152 | bytes 3444736 | tf_op jit(solution)/shard_map/dot_general | solution.py:18
  138.7 0.3 reduce-scatter.5.cloned.1.call-start
  138.9 2.8 %convolution_convert_fusion = bf16[1024,768]{0,1:T(8,128)(2,1)} fusion(bf16[64,768]{1,0:T(8,128)(2,1)} %fusion, s32[1024]{0:T(1024)S(1)} %copy-done.1), kind=kOutput, calls=%fused_computation.2 | convolution fusion | flops 101515264 | bytes 1675264 | tf_op jit(solution)/shard_map/dot_general | solution.py:14
  141.7 3.3 %copy.25 = bf16[1024,8,96]{2,1,0:T(8,128)(2,1)S(1)} copy(bf16[1024,8,96]{0,2,1:T(8,128)(2,1)} %bitcast.31) | data formatting | bytes 3145728 | tf_op jit(solution)/shard_map/reshape | solution.py:46
  145.0 13.6 %broadcast_multiply_fusion = f32[1024,8,96]{2,1,0:T(8,128)} fusion(f32[1024]{0:T(1024)S(1)} %convert_element_type.36, bf16[1024,8,96]{2,1,0:T(8,128)(2,1)S(1)} %copy.25, bf16[1024,96,96]{2,1,0:T(8,128)(2,1)} %copy.17), kind=kOutput, calls=%fused_computation | convolution fusion | flops 151781376 | bytes 23597056 | tf_op jit(solution)/shard_map/kij,kri->krj/dot_general | solution.py:48
  158.5 3.9 %copy.27 = f32[1024,8,96]{0,2,1:T(8,128)S(1)} copy(f32[1024,8,96]{2,1,0:T(8,128)} %broadcast_multiply_fusion) | data formatting | bytes 6291456 | tf_op jit(solution)/shard_map/mul | solution.py:48
  162.4 2.0 fusion.5
  164.4 3.4 %fusion.2 = f32[1024,768]{1,0:T(8,128)} fusion(f32[256,768]{1,0:T(8,128)S(1)} %fusion.5, s32[256]{0:T(256)S(1)} %add.26), kind=kOutput, calls=%fused_computation.13 | convolution fusion | flops 2416181248 | bytes 3933184 | tf_op jit(solution)/shard_map/dot_general | solution.py:18
  167.8 9.6 %all-gather.5.cloned.1.call-done = bf16[1024,768]{1,0:T(8,128)(2,1)} async-done(((bf16[64,768]{1,0:T(8,128)(2,1)}), bf16[1024,768]{1,0:T(8,128)(2,1)}) %all-gather.5.cloned.1.call-update) | async-done | bytes 1572880 | tf_op jit(solution)/shard_map/all_gather | solution.py:52
  177.5 4.0 %convolution_convert_fusion.2 = bf16[1024,768]{0,1:T(8,128)(2,1)} fusion(bf16[1024,768]{1,0:T(8,128)(2,1)} %all-gather.5.cloned.1.call-done, s32[256]{0:T(256)S(1)} %add.26, s32[1024]{0:T(1024)S(1)} %copy-done.2), kind=kOutput, calls=%fused_computation.4 | convolution fusion | flops 806813696 | bytes 3150848 | tf_op jit(solution)/shard_map/dot_general | solution.py:14
  181.5 3.3 %copy.22 = bf16[1024,8,96]{2,1,0:T(8,128)(2,1)S(1)} copy(bf16[1024,8,96]{0,2,1:T(8,128)(2,1)} %bitcast.32) | data formatting | bytes 3145728 | tf_op jit(solution)/shard_map/reshape | solution.py:54
  184.8 18.1 %fusion.27 = f32[1024,8,96]{2,1,0:T(8,128)} fusion(bf16[1024,8,96]{2,1,0:T(8,128)(2,1)S(1)} %copy.22, bf16[1024,96,96]{2,1,0:T(8,128)(2,1)} %copy.17), kind=kOutput, calls=%fused_computation.35 | convolution fusion | flops 150994944 | bytes 23592960 | tf_op jit(solution)/shard_map/kij,krj->kri/dot_general | solution.py:55
  202.9 3.9 %copy.24 = f32[1024,8,96]{0,2,1:T(8,128)S(1)} copy(f32[1024,8,96]{2,1,0:T(8,128)} %fusion.27) | data formatting | bytes 6291456 | tf_op jit(solution)/shard_map/kij,krj->kri/dot_general | solution.py:55
  206.7 39.6 %reduce-scatter.5.cloned.1.call-done = f32[64,768]{1,0:T(8,128)} async-done(((f32[1024,768]{1,0:T(8,128)}), f32[64,768]{1,0:T(8,128)}) %reduce-scatter.5.cloned.1.call-update) | async-done | bytes 196624 | tf_op jit(solution)/shard_map/reduce_scatter | solution.py:58
  246.3 3.5 %fusion.1 = bf16[64,768]{1,0:T(8,128)(2,1)} fusion(f32[64,768]{1,0:T(8,128)} %reduce-scatter.5.cloned.1.call-done, f32[1024,768]{0,1:T(8,128)S(1)} %bitcast.29, s32[1024]{0:T(1024)S(1)} %copy-done.1), kind=kOutput, calls=%fused_computation.11 | convolution fusion | flops 604209152 | bytes 3444736 | tf_op jit(solution)/shard_map/dot_general | solution.py:18
  (19 shorter events, 0.2 us)
Async XLA Ops:
  7.2 59.0 %all-gather.3.cloned.1.call-start = ((), (), s32[]{:S(2)}) async-start(), calls=%async_computation.2 | async-start | bytes 1671168 | tf_op jit(solution)/shard_map/all_gather | solution.py:52
  7.9 29.7 %copy-start.4 = (s32[1024]{0:T(1024)S(1)}, s32[1024]{0:T(1024)}, u32[]{:S(2)}) copy-start(s32[1024]{0:T(1024)} %param.10) | copy-start | bytes 12292
  7.9 29.7 %copy-start = (bf16[64,768]{1,0:T(8,128)(2,1)S(1)}, bf16[64,768]{1,0:T(8,128)(2,1)}, u32[]{:S(2)}) copy-start(bf16[64,768]{1,0:T(8,128)(2,1)} %param.6) | copy-start | bytes 294916
  7.9 29.7 %copy-start.1 = (s32[1024]{0:T(1024)S(1)}, s32[1024]{0:T(1024)}, u32[]{:S(2)}) copy-start(s32[1024]{0:T(1024)} %param.8) | copy-start | bytes 12292
  7.9 127.2 %reduce-scatter.3.cloned.1.call-start = ((), (), s32[]{:S(2)}) async-start(), calls=%async_computation.3 | async-start | bytes 3342336 | tf_op jit(solution)/shard_map/reduce_scatter | solution.py:58
  56.4 4.1 %copy-start.3 = (s32[1,16,16]{2,1,0:T(8,128)S(1)}, s32[1,16,16]{2,1,0:T(8,128)}, u32[]{:S(2)}) copy-start(s32[1,16,16]{2,1,0:T(8,128)} %param.11) | copy-start | bytes 3076
  56.4 4.1 %copy-start.2 = (s32[1024]{0:T(1024)S(1)}, s32[1024]{0:T(1024)}, u32[]{:S(2)}) copy-start(s32[1024]{0:T(1024)} %param.9) | copy-start | bytes 12292
  66.0 111.5 %all-gather.5.cloned.1.call-start = ((), (), s32[]{:S(2)}) async-start(), calls=%async_computation.4 | async-start | bytes 1671168 | tf_op jit(solution)/shard_map/all_gather | solution.py:52
  138.7 107.6 %reduce-scatter.5.cloned.1.call-start = ((), (), s32[]{:S(2)}) async-start(), calls=%async_computation.5 | async-start | bytes 3342336 | tf_op jit(solution)/shard_map/reduce_scatter | solution.py:58
Sparse Core Ops, SparseCore 0:
  10.3 42.3 all-gather.2
  66.1 69.0 reduce-scatter.2
  138.8 38.6 all-gather.4
  181.1 65.1 reduce-scatter.4
where the time goes:
time: 258 us; the launch traced here: 256 us
  matrix products  93.9 us (36%)
  waiting for transfers between devices  89.6 us (35%)
  local copies, waits for them, and re-layouts  58.4 us (23%)
  between operations  13.9 us (5%)
    reduce_scatter x2, waiting for transfers between devices, operate(): lax.psum_scatter(dense_part, 'row', scatter_dimension=0, tiled=True)  79.2 us
    dot_general x2, matrix products, operate(): jnp.einsum('kij,krj->kri', tiles, far_forces, preferred_element_type=jnp....  36.2 us
    unnamed x11, local copies, waits for them, and re-layouts  29.6 us
    dot_general x2, matrix products, operate(): jnp.einsum('kij,kri->krj', tiles, own_forces, preferred_element_type=jnp....  27.1 us
    dot_general x6, matrix products, sum_rows(): lax.dot_general(table, partial_rows, (((0,), (0,)), ((), ())), precision=...  17.8 us
    dot_general x4, matrix products, pick_rows(): jnp.dot(table, values, preferred_element_type=jnp.float32)  12.8 us
    all_gather x2, waiting for transfers between devices, operate(): all_rows = lax.all_gather(current, 'row', axis=0, tiled=True)  9.66 us
    mul x2, local copies, waits for them, and re-layouts, operate(): jnp.einsum('kij,kri->krj', tiles, own_forces, preferred_element_type=jnp....  7.74 us
  transfers between devices with their start and end apart: 4, of which 3 were waited for; matrix products, arithmetic and copies ran while one was open for 57% of the time, Pallas kernels for 0%

commit v1 on v0

v1 whole, which is shorter than its diff:
```python
import functools

import jax
import jax.numpy as jnp
from jax import lax
from jax.experimental import pallas as pl
from jax.experimental.pallas import tpu as pltpu
from jax.sharding import PartitionSpec as P

NRHS = 8
LANES = 128
PAIRS_PER_STEP = 32
QUADS_PER_LOOP = 4
VMEM_LIMIT = 40 * 1024 * 1024


def mirror_kernel(first, unknowns, slots, own_at, slot_at, tile_ref, field_ref, *rest):
    if first:
        slot_ref, wide_ref, near_ref, sum_ref = rest
    else:
        slot_ref, near_ref, sum_ref = rest
    step = pl.program_id(0)
    fibres = field_ref.shape[0]
    depth = 2 * unknowns

    @pl.when(step == 0)
    def _():
        sum_ref[...] = jnp.zeros_like(sum_ref)
        field = field_ref[...].astype(jnp.float32)
        blank = jnp.zeros((fibres, unknowns), jnp.float32)
        for r in range(NRHS):
            part = field[:, r * unknowns : (r + 1) * unknowns]
            near_ref[:fibres, r, :] = jnp.concatenate([part, blank], axis=1)
            near_ref[fibres:, r, :] = jnp.concatenate([blank, part], axis=1)

    def quads(loop, carry):
        found = []
        for u in range(QUADS_PER_LOOP):
            pair = (loop * QUADS_PER_LOOP + u) * 2
            tile = (step * PAIRS_PER_STEP + pair) * 2
            halves = []
            for h in range(2):
                half = tile_ref[pair + h]
                if first:
                    half = jnp.concatenate(
                        [half, jnp.zeros((depth, LANES - unknowns), half.dtype)], axis=1
                    )
                    wide_ref[pair + h] = half
                halves.append(half)
            left = jnp.concatenate(
                [near_ref[own_at[tile + t]] for t in range(4)], axis=0
            ).astype(jnp.bfloat16)
            right = jnp.concatenate(halves, axis=1)
            found.append(jnp.dot(left, right, preferred_element_type=jnp.float32))
        for u in range(QUADS_PER_LOOP):
            tile = (step * PAIRS_PER_STEP + (loop * QUADS_PER_LOOP + u) * 2) * 2
            for t in range(4):
                lane = (t // 2) * LANES
                slot = slot_at[tile + t]
                sum_ref[slot] += found[u][t * NRHS : (t + 1) * NRHS, lane : lane + LANES]
        return carry

    lax.fori_loop(0, PAIRS_PER_STEP // (2 * QUADS_PER_LOOP), quads, 0)

    @pl.when(step == pl.num_programs(0) - 1)
    def _():
        rows = [sum_ref[:slots, r, :][:, :unknowns] for r in range(NRHS)]
        slot_ref[...] = jnp.concatenate(rows, axis=1).astype(slot_ref.dtype)


def mirror(first, tiles, field, own_at, slot_at, slots):
    pairs, depth, width = tiles.shape
    unknowns = depth // 2
    fibres = field.shape[0]
    steps = pairs // PAIRS_PER_STEP
    tile_spec = pl.BlockSpec((PAIRS_PER_STEP, depth, width), lambda i, *_: (i, 0, 0))
    wide_spec = pl.BlockSpec((PAIRS_PER_STEP, depth, LANES), lambda i, *_: (i, 0, 0))
    out_shape = [jax.ShapeDtypeStruct((slots, field.shape[1]), jnp.bfloat16)]
    out_specs = [pl.BlockSpec((slots, field.shape[1]), lambda i, *_: (0, 0))]
    if first:
        out_shape.append(jax.ShapeDtypeStruct((pairs, depth, LANES), tiles.dtype))
        out_specs.append(wide_spec)
    return pl.pallas_call(
        functools.partial(mirror_kernel, first, unknowns, slots),
        out_shape=out_shape,
        grid_spec=pltpu.PrefetchScalarGridSpec(
            num_scalar_prefetch=2,
            grid=(steps,),
            in_specs=[tile_spec, pl.BlockSpec(field.shape, lambda i, *_: (0, 0))],
            out_specs=out_specs,
            scratch_shapes=[
                pltpu.VMEM((2 * fibres, NRHS, depth), jnp.float32),
                pltpu.VMEM((slots + 1, NRHS, LANES), jnp.float32),
            ],
        ),
        compiler_params=pltpu.CompilerParams(vmem_limit_bytes=VMEM_LIMIT),
        cost_estimate=pl.CostEstimate(
            flops=4 * pairs * depth * NRHS * unknowns,
            bytes_accessed=2 * pairs * depth * LANES * (2 if first else 1),
            transcendentals=0,
        ),
        name="mirror_first" if first else "mirror",
    )(own_at, slot_at, tiles, field)


def direct_kernel(unknowns, own_at, slot_at, tile_ref, field_ref, own_ref, far_ref, even_ref, odd_ref):
    step = pl.program_id(0)
    slots = field_ref.shape[0]

    @pl.when(step == 0)
    def _():
        even_ref[...] = jnp.zeros_like(even_ref)
        odd_ref[...] = jnp.zeros_like(odd_ref)
        field = field_ref[...].astype(jnp.float32)
        blank = jnp.zeros((slots, LANES - unknowns), jnp.float32)
        for r in range(NRHS):
            part = field[:, r * unknowns : (r + 1) * unknowns]
            far_ref[:, r, :] = jnp.concatenate([part, blank], axis=1)

    none = jnp.zeros((NRHS, LANES), jnp.float32)

    def quads(loop, carry):
        found = []
        for u in range(QUADS_PER_LOOP):
            pair = (loop * QUADS_PER_LOOP + u) * 2
            tile = (step * PAIRS_PER_STEP + pair) * 2
            far = [far_ref[slot_at[tile + t]] for t in range(4)]
            left = jnp.concatenate(
                [
                    jnp.concatenate(far[:2] + [none, none], axis=0),
                    jnp.concatenate([none, none] + far[2:], axis=0),
                ],
                axis=1,
            ).astype(jnp.bfloat16)
            right = jnp.concatenate([tile_ref[pair], tile_ref[pair + 1]], axis=1)
            found.append(
                lax.dot_general(
                    left, right, (((1,), (1,)), ((), ())), preferred_element_type=jnp.float32
                )
            )
        for u in range(QUADS_PER_LOOP):
            tile = (step * PAIRS_PER_STEP + (loop * QUADS_PER_LOOP + u) * 2) * 2
            for t in range(4):
                rows = found[u][t * NRHS : (t + 1) * NRHS]
                own = own_at[tile + t]
                if t % 2 == 0:
                    even_ref[own] += rows[:, :LANES]
                else:
                    odd_ref[own] += rows
        return carry

    lax.fori_loop(0, PAIRS_PER_STEP // (2 * QUADS_PER_LOOP), quads, 0)

    @pl.when(step == pl.num_programs(0) - 1)
    def _():
        rows = [
            even_ref[:, r, :][:, :unknowns] + odd_ref[:, r, :][:, unknowns:]
            for r in range(NRHS)
        ]
        own_ref[...] = jnp.concatenate(rows, axis=1)


def direct(tiles, field, own_at, slot_at, fibres):
    pairs, depth, width = tiles.shape
    unknowns = depth // 2
    slots = field.shape[0]
    return pl.pallas_call(
        functools.partial(direct_kernel, unknowns),
        out_shape=jax.ShapeDtypeStruct((fibres, field.shape[1]), jnp.float32),
        grid_spec=pltpu.PrefetchScalarGridSpec(
            num_scalar_prefetch=2,
            grid=(pairs // PAIRS_PER_STEP,),
            in_specs=[
                pl.BlockSpec((PAIRS_PER_STEP, depth, width), lambda i, *_: (i, 0, 0)),
                pl.BlockSpec(field.shape, lambda i, *_: (0, 0)),
            ],
            out_specs=pl.BlockSpec((fibres, field.shape[1]), lambda i, *_: (0, 0)),
            scratch_shapes=[
                pltpu.VMEM((slots, NRHS, LANES), jnp.float32),
                pltpu.VMEM((fibres, NRHS, LANES), jnp.float32),
                pltpu.VMEM((fibres, NRHS, depth), jnp.float32),
            ],
        ),
        compiler_params=pltpu.CompilerParams(vmem_limit_bytes=VMEM_LIMIT),
        cost_estimate=pl.CostEstimate(
            flops=4 * pairs * depth * NRHS * unknowns,
            bytes_accessed=2 * pairs * depth * LANES,
            transcendentals=0,
        ),
        name="direct",
    )(own_at, slot_at, tiles, field)


def per_device(forces, tiles, tile_local, tile_slot, tile_flag, want_list):
    fibres, row_width = forces.shape
    blocks, unknowns, _ = tiles.shape
    _, peers, capacity = want_list.shape
    slots = peers * capacity

    def exchange(rows):
        return lax.all_to_all(rows, "row", 0, 0)

    asked = exchange(want_list[0]).reshape(slots)
    asked_pick = (asked[:, None] == jnp.arange(fibres, dtype=jnp.int32)[None, :]).astype(
        jnp.bfloat16
    )
    mirror_own = tile_local + fibres * (jnp.arange(blocks, dtype=jnp.int32) % 2)
    mirror_slot = jnp.where(tile_flag == 1, tile_slot, slots)

    def fetch(current):
        rows = jnp.dot(asked_pick, current, preferred_element_type=jnp.float32)
        rows = rows.astype(jnp.bfloat16).reshape(peers, capacity, row_width)
        return exchange(rows).reshape(slots, row_width)

    def give_back(slot_part):
        back = exchange(slot_part.reshape(peers, capacity, row_width)).reshape(slots, row_width)
        return lax.dot_general(
            asked_pick, back, (((0,), (0,)), ((), ())), preferred_element_type=jnp.float32
        )

    far = fetch(forces)
    slot_part, wide = mirror(
        True, tiles.reshape(blocks // 2, 2 * unknowns, unknowns), forces, mirror_own, mirror_slot, slots
    )
    own_part = direct(wide, far, tile_local, tile_slot, fibres)
    krylov_one = (own_part + give_back(slot_part)).astype(jnp.bfloat16)

    far = fetch(krylov_one)
    (slot_part,) = mirror(False, wide, krylov_one, mirror_own, mirror_slot, slots)
    own_part = direct(wide, far, tile_local, tile_slot, fibres)
    krylov_two = (own_part + give_back(slot_part)).astype(jnp.bfloat16)
    return (krylov_one, krylov_two)


def solution(mesh):
    spec = ("groups", "row")
    in_specs = (
        P(spec, None),
        P(spec, None, None),
        P(spec),
        P(spec),
        P(spec),
        P(spec, None, None),
    )
    out_specs = (P(spec, None), P(spec, None))
    return jax.shard_map(
        per_device, mesh=mesh, in_specs=in_specs, out_specs=out_specs, check_vma=False
    )
```

time: 258 us -> 171 us (0.66)
  Pallas kernels: 0 us -> 97.6 us
  matrix products: 93.9 us -> 4.31 us
  waiting for transfers between devices: 89.6 us -> 0.01 us
  local copies, waits for them, and re-layouts: 58.4 us -> 30.2 us
  starting transfers between devices: 0.56 us -> 21.6 us
  blocking collectives: 0 us -> 13.9 us
  between operations: 13.9 us -> 0.77 us
    pallas_call x0 -> x4, Pallas kernels: none -> 97.6 us  [the longest x2 51.1 us: mirror(): pl.pallas_call(functools.partial(mirror_kernel, first, unknowns, slots),...]
    dot_general x14 -> x4, matrix products: 93.9 us -> 4.31 us  [the longest x2 3.06 us: fetch(): rows = jnp.dot(asked_pick, current, preferred_element_type=jnp.float32)]
    reduce_scatter x2 -> x0, waiting for transfers between devices: 79.2 us -> none  [operate(): lax.psum_scatter(dense_part, 'row', scatter_dimension=0, tiled=True)]
    all_to_all x0 -> x4, starting transfers between devices: none -> 21.6 us  [exchange(): return lax.all_to_all(rows, 'row', 0, 0)]
    all_to_all x0 -> x1, blocking collectives: none -> 13.9 us  [exchange(): return lax.all_to_all(rows, 'row', 0, 0)]
    reshape x4 -> x0, local copies, waits for them, and re-layouts: 13.1 us -> none  [the longest x2 6.54 us: operate(): own_forces = pick_rows(local_pick, current).reshape(blocks, NRHS, unknowns)]
    all_gather x2 -> x0, waiting for transfers between devices: 9.66 us -> none  [operate(): all_rows = lax.all_gather(current, 'row', axis=0, tiled=True)]
    mul x2 -> x0, local copies, waits for them, and re-layouts: 7.74 us -> none  [operate(): jnp.einsum('kij,kri->krj', tiles, own_forces, preferred_element_type=jnp....]
  transfers between devices with their start and end apart: 4 -> 4, of which waited for: 3 -> 0; matrix products, arithmetic and copies ran while one was open for 57% -> 18% of each run, Pallas kernels for 0% -> 58%
where the time goes in v1:
time: 171 us; the launch traced here: 169 us
  Pallas kernels  97.6 us (57%)
  local copies, waits for them, and re-layouts  30.2 us (18%)
  starting transfers between devices  21.6 us (13%)
  blocking collectives  13.9 us (8%)
  matrix products  4.31 us (3%)
    pallas_call x2, Pallas kernels, mirror(): pl.pallas_call(functools.partial(mirror_kernel, first, unknowns, slots),...  51.1 us
    pallas_call x2, Pallas kernels, direct(): pl.pallas_call(functools.partial(direct_kernel, unknowns), out_shape=jax....  46.5 us
    unnamed x11, local copies, waits for them, and re-layouts  29.6 us
    all_to_all x4, starting transfers between devices, exchange(): return lax.all_to_all(rows, 'row', 0, 0)  21.6 us
    all_to_all x1, blocking collectives, exchange(): return lax.all_to_all(rows, 'row', 0, 0)  13.9 us
  transfers between devices with their start and end apart: 4, of which 0 were waited for; matrix products, arithmetic and copies ran while one was open for 18% of the time, Pallas kernels for 58%

profile of v1, /device:TPU:0, one launch (start us, length us, event | category | flops | bytes accessed | tf_op | source)
XLA Modules:
  0.0 169.1 jit_solution(7209132483768830018)
XLA Ops:
  0.6 0.0 copy-start.1
  0.6 0.0 copy-start.4
  0.7 0.0 copy-start.2
  0.7 0.0 copy-start.3
  0.7 13.9 %all_to_all.29 = s32[16,1,16]{2,1,0:T(1,128)S(1)} all-to-all(s32[16,1,16]{2,1,0:T(1,128)} %bitcast.19), channel_id=1, replica_groups=mesh['groups'=2,'row'=16] {'row'}, dimensions={0} | all-to-all | bytes 2048 | tf_op jit(solution)/shard_map/all_to_all | solution.py:201
  14.5 0.5 broadcast.8
  15.0 0.7 reduce.3
  15.7 0.1 eq.22
  15.8 2.0 %convolution_convert_fusion.1 = bf16[256,768]{1,0:T(8,128)(2,1)} fusion(bf16[64,768]{1,0:T(8,128)(2,1)} %field_ref.1, s32[256]{0:T(256)S(1)} %eq.22), kind=kOutput, calls=%fused_computation.1 | convolution fusion | flops 25378816 | bytes 492544 | tf_op jit(solution)/shard_map/dot_general | solution.py:211
  17.8 3.6 %all-to-all-start.1 = ((bf16[16,16,768]{2,1,0:T(8,128)(2,1)}), bf16[16,16,768]{2,1,0:T(8,128)(2,1)S(1)}, u32[]{:S(2)}, u32[]{:S(2)}) async-start(bf16[16,16,768]{2,1,0:T(8,128)(2,1)} %bitcast.2), calls=%async_computation.1 | async-start | bytes 786432 | tf_op jit(solution)/shard_map/all_to_all | solution.py:201
  21.3 29.6 %copy.9 = bf16[1024,96,96]{2,1,0:T(8,128)(2,1)} copy(bf16[1024,96,96]{0,2,1:T(8,128)(2,1)} %param.7) | data formatting | bytes 37748736 | tf_op args[1]
  51.0 0.0 copy-done.4
  51.0 0.0 copy-done.2
  51.0 0.0 copy-done.3
  51.0 0.0 copy-done.1
  51.0 29.0 %mirror_first.1 = (bf16[256,768]{1,0:T(8,128)(2,1)}, bf16[512,192,128]{2,1,0:T(8,128)(2,1)}) custom-call(s32[1024]{0:T(1024)S(1)} %get-tuple-element.6.own_at, s32[1024]{0:T(1024)S(1)} %get-tuple-element.7.slot_at, bf16[512,192,96]{2,1,0:T(8,128)(2,1)} %bitcast.16, bf16[64,768]{1,0:T(8,128)(2,1)S(1)} %copy-done.1), custom_call_target="tpu_custom_call" | custom-call | flops 301989888 | bytes 50331648 | tf_op jit(solution)/shard_map/mirror_first/pallas_call | solution.py:83
  80.0 0.0 all-to-all-done.1
  80.0 6.1 %all-to-all-start.2 = ((bf16[16,16,768]{2,1,0:T(8,128)(2,1)}), bf16[16,16,768]{2,1,0:T(8,128)(2,1)S(1)}, u32[]{:S(2)}, u32[]{:S(2)}) async-start(bf16[16,16,768]{2,1,0:T(8,128)(2,1)} %bitcast.4), calls=%async_computation.2 | async-start | bytes 786432 | tf_op jit(solution)/shard_map/all_to_all | solution.py:201
  86.1 23.2 %direct.2 = f32[64,768]{1,0:T(8,128)S(1)} custom-call(s32[1024]{0:T(1024)S(1)} %copy-done.2, s32[1024]{0:T(1024)S(1)} %copy-done.3, bf16[512,192,128]{2,1,0:T(8,128)(2,1)} %get-tuple-element.4.tile_ref, bf16[256,768]{1,0:T(8,128)(2,1)S(1)} %bitcast.14), custom_call_target="tpu_custom_call" | custom-call | flops 301989888 | bytes 25165824 | tf_op jit(solution)/shard_map/direct/pallas_call | solution.py:167
  109.3 0.0 all-to-all-done.2
  109.4 0.3 fusion.field_ref
  109.7 0.0 copy-start
  109.7 1.1 convolution_convert_fusion
  110.8 6.0 %all-to-all-start.3 = ((bf16[16,16,768]{2,1,0:T(8,128)(2,1)}), bf16[16,16,768]{2,1,0:T(8,128)(2,1)S(1)}, u32[]{:S(2)}, u32[]{:S(2)}) async-start(bf16[16,16,768]{2,1,0:T(8,128)(2,1)} %bitcast.6), calls=%async_computation.3 | async-start | bytes 786432 | tf_op jit(solution)/shard_map/all_to_all | solution.py:201
  116.8 22.1 %mirror.1 = bf16[256,768]{1,0:T(8,128)(2,1)} custom-call(s32[1024]{0:T(1024)S(1)} %get-tuple-element.6.own_at, s32[1024]{0:T(1024)S(1)} %get-tuple-element.7.slot_at, bf16[512,192,128]{2,1,0:T(8,128)(2,1)} %get-tuple-element.4.tile_ref, bf16[64,768]{1,0:T(8,128)(2,1)S(1)} %fusion.field_ref), custom_call_target="tpu_custom_call" | custom-call | flops 301989888 | bytes 25165824 | tf_op jit(solution)/shard_map/mirror/pallas_call | solution.py:83
  138.8 0.0 all-to-all-done.3
  138.8 6.0 %all-to-all-start.4 = ((bf16[16,16,768]{2,1,0:T(8,128)(2,1)}), bf16[16,16,768]{2,1,0:T(8,128)(2,1)S(1)}, u32[]{:S(2)}, u32[]{:S(2)}) async-start(bf16[16,16,768]{2,1,0:T(8,128)(2,1)} %bitcast.8), calls=%async_computation.4 | async-start | bytes 786432 | tf_op jit(solution)/shard_map/all_to_all | solution.py:201
  144.8 23.2 %direct.3 = f32[64,768]{1,0:T(8,128)S(1)} custom-call(s32[1024]{0:T(1024)S(1)} %copy-done.2, s32[1024]{0:T(1024)S(1)} %copy-done.3, bf16[512,192,128]{2,1,0:T(8,128)(2,1)} %get-tuple-element.4.tile_ref, bf16[256,768]{1,0:T(8,128)(2,1)S(1)} %bitcast.15), custom_call_target="tpu_custom_call" | custom-call | flops 301989888 | bytes 25165824 | tf_op jit(solution)/shard_map/direct/pallas_call | solution.py:167
  168.1 0.0 copy-done
  168.1 0.0 all-to-all-done.4
  168.1 0.9 fusion.1
  (1 shorter events, 0.0 us)
Async XLA Ops:
  0.6 50.3 %copy-start.1 = (bf16[64,768]{1,0:T(8,128)(2,1)S(1)}, bf16[64,768]{1,0:T(8,128)(2,1)}, u32[]{:S(2)}) copy-start(bf16[64,768]{1,0:T(8,128)(2,1)} %field_ref.1) | copy-start | bytes 294916
  0.6 50.3 %copy-start.4 = (s32[1024]{0:T(1024)S(1)}, s32[1024]{0:T(1024)}, u32[]{:S(2)}) copy-start(s32[1024]{0:T(1024)} %param.10) | copy-start | bytes 12292
  0.7 50.3 %copy-start.2 = (s32[1024]{0:T(1024)S(1)}, s32[1024]{0:T(1024)}, u32[]{:S(2)}) copy-start(s32[1024]{0:T(1024)} %own_at.3) | copy-start | bytes 12292
  0.7 50.3 %copy-start.3 = (s32[1024]{0:T(1024)S(1)}, s32[1024]{0:T(1024)}, u32[]{:S(2)}) copy-start(s32[1024]{0:T(1024)} %slot_at.3) | copy-start | bytes 12292
  17.8 62.3 %all-to-all-start.1 = ((bf16[16,16,768]{2,1,0:T(8,128)(2,1)}), bf16[16,16,768]{2,1,0:T(8,128)(2,1)S(1)}, u32[]{:S(2)}, u32[]{:S(2)}) async-start(bf16[16,16,768]{2,1,0:T(8,128)(2,1)} %bitcast.2), calls=%async_computation.1 | async-start | bytes 786432 | tf_op jit(solution)/shard_map/all_to_all | solution.py:201
  80.0 29.3 %all-to-all-start.2 = ((bf16[16,16,768]{2,1,0:T(8,128)(2,1)}), bf16[16,16,768]{2,1,0:T(8,128)(2,1)S(1)}, u32[]{:S(2)}, u32[]{:S(2)}) async-start(bf16[16,16,768]{2,1,0:T(8,128)(2,1)} %bitcast.4), calls=%async_computation.2 | async-start | bytes 786432 | tf_op jit(solution)/shard_map/all_to_all | solution.py:201
  109.7 58.4 %copy-start = (bf16[64,768]{1,0:T(8,128)(2,1)}, bf16[64,768]{1,0:T(8,128)(2,1)S(1)}, u32[]{:S(2)}) copy-start(bf16[64,768]{1,0:T(8,128)(2,1)S(1)} %fusion.field_ref) | copy-start | bytes 294916
  110.8 28.1 %all-to-all-start.3 = ((bf16[16,16,768]{2,1,0:T(8,128)(2,1)}), bf16[16,16,768]{2,1,0:T(8,128)(2,1)S(1)}, u32[]{:S(2)}, u32[]{:S(2)}) async-start(bf16[16,16,768]{2,1,0:T(8,128)(2,1)} %bitcast.6), calls=%async_computation.3 | async-start | bytes 786432 | tf_op jit(solution)/shard_map/all_to_all | solution.py:201
  138.8 29.3 %all-to-all-start.4 = ((bf16[16,16,768]{2,1,0:T(8,128)(2,1)}), bf16[16,16,768]{2,1,0:T(8,128)(2,1)S(1)}, u32[]{:S(2)}, u32[]{:S(2)}) async-start(bf16[16,16,768]{2,1,0:T(8,128)(2,1)} %bitcast.8), calls=%async_computation.4 | async-start | bytes 786432 | tf_op jit(solution)/shard_map/all_to_all | solution.py:201

commit v2 on v0

v2 whole, which is shorter than its diff:
```python
import jax
import jax.numpy as jnp
from jax import lax
from jax.experimental import pallas as pl
from jax.experimental.pallas import tpu as pltpu
from jax.sharding import PartitionSpec as P

NRHS = 8
LANES = 128
QUADS_PER_LOOP = 16
NOTE_ROWS = 16
PAIRS_PER_CHUNK = 64
CHUNKS_HELD = 3
STRIDE_PAD = 1
RELAY_LOOPS = 4
TILE_BLOCK = 128
RELAY_VMEM = 26 * 1024 * 1024
PRODUCT_VMEM = 20 * 1024 * 1024


def relay_kernel(native_ref, wide_ref, line_ref):
    step = pl.program_id(0)
    last = pl.num_programs(0) - 1
    unknowns = native_ref.shape[0]
    block = native_ref.shape[2]
    stride = block + STRIDE_PAD
    lines = unknowns * stride
    put_at = (step % 2) * lines
    take_at = ((step + 1) % 2) * lines
    blank = jnp.zeros((LANES - unknowns, block), native_ref.dtype)
    rows = unknowns // RELAY_LOOPS
    pairs = block // (2 * RELAY_LOOPS)

    def turn(loop):
        for u in range(rows):
            i = loop * rows + u
            wide = jnp.concatenate([native_ref[i], blank], axis=0)
            line_ref[pl.ds(put_at + i * stride, block), :] = wide.T.astype(jnp.float32)

    def collect(loop):
        for u in range(pairs):
            pair = loop * pairs + u
            for h in range(2):
                lines_of = pl.ds(take_at + 2 * pair + h, unknowns, stride=stride)
                wide_ref[pair, h * unknowns : (h + 1) * unknowns, :] = line_ref[
                    lines_of, :
                ].astype(wide_ref.dtype)

    def run(*parts):
        def body(loop, carry):
            for part in parts:
                part(loop)
            return carry

        lax.fori_loop(0, RELAY_LOOPS, body, 0)

    @pl.when(step == 0)
    def _():
        run(turn)

    @pl.when(jnp.logical_and(step > 0, step < last))
    def _():
        run(collect, turn)

    @pl.when(step == last)
    def _():
        run(collect)


def relay(native):
    unknowns, _, blocks = native.shape
    steps = blocks // TILE_BLOCK
    return pl.pallas_call(
        relay_kernel,
        out_shape=pltpu.HBM((blocks // 2, 2 * unknowns, LANES), native.dtype),
        grid=(steps + 1,),
        in_specs=[
            pl.BlockSpec(
                (unknowns, unknowns, TILE_BLOCK), lambda i: (0, 0, jnp.minimum(i, steps - 1))
            )
        ],
        out_specs=pl.BlockSpec(
            (TILE_BLOCK // 2, 2 * unknowns, LANES), lambda i: (jnp.maximum(i - 1, 0), 0, 0)
        ),
        scratch_shapes=[
            pltpu.VMEM((2 * unknowns * (TILE_BLOCK + STRIDE_PAD), LANES), jnp.float32)
        ],
        compiler_params=pltpu.CompilerParams(vmem_limit_bytes=RELAY_VMEM),
        cost_estimate=pl.CostEstimate(
            flops=0, bytes_accessed=8 * blocks * unknowns * LANES, transcendentals=0
        ),
        name="relay",
    )(pltpu.with_memory_space_constraint(native, pltpu.HBM))


def chunk_copy(tile_ref, held_ref, ready, chunk):
    slot = chunk % CHUNKS_HELD
    return pltpu.make_async_copy(
        tile_ref.at[pl.ds(chunk * PAIRS_PER_CHUNK, PAIRS_PER_CHUNK)],
        held_ref.at[slot],
        ready.at[slot],
    )


def open_stream(tile_ref, held_ref, ready):
    for chunk in range(CHUNKS_HELD - 1):
        chunk_copy(tile_ref, held_ref, ready, chunk).start()


def run_stream(tile_ref, held_ref, ready, quads):
    chunks = tile_ref.shape[0] // PAIRS_PER_CHUNK

    def body(chunk, carry):
        chunk_copy(tile_ref, held_ref, ready, chunk).wait()

        @pl.when(chunk + CHUNKS_HELD - 1 < chunks)
        def _():
            chunk_copy(tile_ref, held_ref, ready, chunk + CHUNKS_HELD - 1).start()

        held = held_ref.at[chunk % CHUNKS_HELD]

        def inner(loop, carry):
            quads(held, loop * 2 * QUADS_PER_LOOP, chunk * PAIRS_PER_CHUNK)
            return carry

        return lax.fori_loop(0, PAIRS_PER_CHUNK // (2 * QUADS_PER_LOOP), inner, carry)

    lax.fori_loop(0, chunks, body, 0)


def mirror_kernel(
    own_at, slot_at, tile_ref, field_ref, slot_ref, held_ref, ready, near_ref, sum_ref
):
    open_stream(tile_ref, held_ref, ready)
    fibres, width = field_ref.shape
    slots = slot_ref.shape[0]
    unknowns = width // NRHS
    sum_ref[...] = jnp.zeros_like(sum_ref)
    field = field_ref[...].astype(jnp.float32)
    blank = jnp.zeros((fibres, unknowns), jnp.float32)
    for r in range(NRHS):
        part = field[:, r * unknowns : (r + 1) * unknowns]
        near_ref[:fibres, r, :] = jnp.concatenate([part, blank], axis=1)
        near_ref[fibres:, r, :] = jnp.concatenate([blank, part], axis=1)

    def quads(held, pair_at, chunk_at):
        first = 2 * (chunk_at + pair_at)
        found = []
        for u in range(QUADS_PER_LOOP):
            pair = pair_at + 2 * u
            left = jnp.concatenate(
                [near_ref[own_at[first + 4 * u + t]] for t in range(4)], axis=0
            ).astype(jnp.bfloat16)
            right = jnp.concatenate([held[pair], held[pair + 1]], axis=1)
            found.append(jnp.dot(left, right, preferred_element_type=jnp.float32))
        for u in range(QUADS_PER_LOOP):
            for t in range(4):
                lane = (t // 2) * LANES
                slot = slot_at[first + 4 * u + t]
                sum_ref[slot] += found[u][t * NRHS : (t + 1) * NRHS, lane : lane + LANES]

    run_stream(tile_ref, held_ref, ready, quads)
    rows = [sum_ref[:slots, r, :][:, :unknowns] for r in range(NRHS)]
    slot_ref[...] = jnp.concatenate(rows, axis=1).astype(slot_ref.dtype)


def product_call(kernel, name, tiles, field, own_at, slot_at, out_shape, scratch_shapes):
    pairs, depth, _ = tiles.shape
    whole = pl.BlockSpec(memory_space=pltpu.VMEM)
    stay = pl.BlockSpec(memory_space=pltpu.HBM)
    stream_shapes = [
        pltpu.VMEM((CHUNKS_HELD, PAIRS_PER_CHUNK, depth, LANES), tiles.dtype),
        pltpu.SemaphoreType.DMA((CHUNKS_HELD,)),
    ]
    index = pl.BlockSpec(memory_space=pltpu.SMEM)
    return pl.pallas_call(
        kernel,
        out_shape=out_shape,
        in_specs=[index, index, stay, whole],
        out_specs=whole,
        scratch_shapes=stream_shapes + scratch_shapes,
        compiler_params=pltpu.CompilerParams(vmem_limit_bytes=PRODUCT_VMEM),
        cost_estimate=pl.CostEstimate(
            flops=4 * pairs * depth * NRHS * LANES,
            bytes_accessed=2 * pairs * depth * LANES,
            transcendentals=0,
        ),
        name=name,
    )(own_at, slot_at, pltpu.with_memory_space_constraint(tiles, pltpu.HBM), field)


def mirror(tiles, field, own_at, slot_at, slots):
    fibres, width = field.shape
    return product_call(
        mirror_kernel,
        "mirror",
        tiles,
        field,
        own_at,
        slot_at,
        jax.ShapeDtypeStruct((slots, width), jnp.bfloat16),
        [
            pltpu.VMEM((2 * fibres, NRHS, tiles.shape[1]), jnp.float32),
            pltpu.VMEM((slots + 1, NRHS, LANES), jnp.float32),
        ],
    )


def direct_kernel(
    own_at, slot_at, tile_ref, field_ref, own_ref, held_ref, ready, far_ref, even_ref, odd_ref
):
    open_stream(tile_ref, held_ref, ready)
    slots, width = field_ref.shape
    unknowns = width // NRHS
    even_ref[...] = jnp.zeros_like(even_ref)
    odd_ref[...] = jnp.zeros_like(odd_ref)
    field = field_ref[...].astype(jnp.float32)
    blank = jnp.zeros((slots, LANES - unknowns), jnp.float32)
    for r in range(NRHS):
        part = field[:, r * unknowns : (r + 1) * unknowns]
        far_ref[:, r, :] = jnp.concatenate([part, blank], axis=1)

    none = jnp.zeros((NRHS, LANES), jnp.float32)

    def quads(held, pair_at, chunk_at):
        first = 2 * (chunk_at + pair_at)
        found = []
        for u in range(QUADS_PER_LOOP):
            pair = pair_at + 2 * u
            far = [far_ref[slot_at[first + 4 * u + t]] for t in range(4)]
            left = jnp.concatenate(
                [
                    jnp.concatenate(far[:2] + [none, none], axis=0),
                    jnp.concatenate([none, none] + far[2:], axis=0),
                ],
                axis=1,
            ).astype(jnp.bfloat16)
            right = jnp.concatenate([held[pair], held[pair + 1]], axis=1)
            found.append(
                lax.dot_general(
                    left, right, (((1,), (1,)), ((), ())), preferred_element_type=jnp.float32
                )
            )
        for u in range(QUADS_PER_LOOP):
            for t in range(4):
                rows = found[u][t * NRHS : (t + 1) * NRHS]
                own = own_at[first + 4 * u + t]
                if t % 2 == 0:
                    even_ref[own] += rows[:, :LANES]
                else:
                    odd_ref[own] += rows

    run_stream(tile_ref, held_ref, ready, quads)
    rows = [
        even_ref[:, r, :][:, :unknowns] + odd_ref[:, r, :][:, unknowns:] for r in range(NRHS)
    ]
    own_ref[...] = jnp.concatenate(rows, axis=1)


def direct(tiles, field, own_at, slot_at, fibres):
    slots, width = field.shape
    return product_call(
        direct_kernel,
        "direct",
        tiles,
        field,
        own_at,
        slot_at,
        jax.ShapeDtypeStruct((fibres, width), jnp.float32),
        [
            pltpu.VMEM((slots, NRHS, LANES), jnp.float32),
            pltpu.VMEM((fibres, NRHS, LANES), jnp.float32),
            pltpu.VMEM((fibres, NRHS, tiles.shape[1]), jnp.float32),
        ],
    )


def per_device(forces, tiles, tile_local, tile_slot, tile_flag, want_list):
    fibres, row_width = forces.shape
    blocks = tiles.shape[0]
    _, peers, capacity = want_list.shape
    slots = peers * capacity

    def exchange(rows):
        return lax.all_to_all(rows, "row", 0, 0)

    me = lax.axis_index("row")
    notes = want_list[0].astype(jnp.bfloat16).reshape(1, slots)
    notes = jnp.pad(notes, ((0, NOTE_ROWS - 1), (0, row_width - slots)))
    everyone = lax.all_gather(jnp.concatenate([forces, notes], axis=0), "row")
    wanted = everyone[:, fibres, :slots].reshape(peers, peers, capacity)
    asked = lax.dynamic_index_in_dim(wanted, me, 1, False).astype(jnp.int32).reshape(slots)
    asked_pick = (asked[:, None] == jnp.arange(fibres, dtype=jnp.int32)[None, :]).astype(
        jnp.bfloat16
    )
    mirror_own = tile_local + fibres * (jnp.arange(blocks, dtype=jnp.int32) % 2)
    mirror_slot = jnp.where(tile_flag == 1, tile_slot, slots)

    def fetch(current):
        rows = jnp.dot(asked_pick, current, preferred_element_type=jnp.float32)
        rows = rows.astype(jnp.bfloat16).reshape(peers, capacity, row_width)
        return exchange(rows).reshape(slots, row_width)

    def give_back(slot_part):
        back = exchange(slot_part.reshape(peers, capacity, row_width)).reshape(slots, row_width)
        return lax.dot_general(
            asked_pick, back, (((0,), (0,)), ((), ())), preferred_element_type=jnp.float32
        )

    wide = relay(tiles.transpose(1, 2, 0))
    rows = (jnp.arange(peers, dtype=jnp.int32)[:, None] * (fibres + NOTE_ROWS) + want_list[0]).reshape(slots)
    spread = jnp.arange(peers * (fibres + NOTE_ROWS), dtype=jnp.int32)
    first_pick = (rows[:, None] == spread[None, :]).astype(jnp.bfloat16)
    far = jnp.dot(
        first_pick, everyone.reshape(-1, row_width), preferred_element_type=jnp.float32
    ).astype(jnp.bfloat16)
    slot_part = mirror(wide, forces, mirror_own, mirror_slot, slots)
    own_part = direct(wide, far, tile_local, tile_slot, fibres)
    krylov_one = (own_part + give_back(slot_part)).astype(jnp.bfloat16)

    far = fetch(krylov_one)
    slot_part = mirror(wide, krylov_one, mirror_own, mirror_slot, slots)
    own_part = direct(wide, far, tile_local, tile_slot, fibres)
    krylov_two = (own_part + give_back(slot_part)).astype(jnp.bfloat16)
    return (krylov_one, krylov_two)


def solution(mesh):
    spec = ("groups", "row")
    in_specs = (
        P(spec, None),
        P(spec, None, None),
        P(spec),
        P(spec),
        P(spec),
        P(spec, None, None),
    )
    out_specs = (P(spec, None), P(spec, None))
    return jax.shard_map(
        per_device, mesh=mesh, in_specs=in_specs, out_specs=out_specs, check_vma=False
    )
```

time: 258 us -> 118 us (0.46)
  matrix products: 93.9 us -> 4.64 us
  waiting for transfers between devices: 89.6 us -> 2.37 us
  Pallas kernels: 0 us -> 74.9 us
  local copies, waits for them, and re-layouts: 58.4 us -> 1.39 us
  starting transfers between devices: 0.56 us -> 17.1 us
    dot_general x14 -> x4, matrix products: 93.9 us -> 4.64 us  [the longest x1 2.28 us: per_device(): jnp.dot(first_pick, everyone.reshape(-1, row_width), preferred_element_ty...]
    reduce_scatter x2 -> x0, waiting for transfers between devices: 79.2 us -> none  [operate(): lax.psum_scatter(dense_part, 'row', scatter_dimension=0, tiled=True)]
    pallas_call x0 -> x5, Pallas kernels: none -> 74.9 us  [the longest x4 53.2 us: product_call(): pl.pallas_call(kernel, out_shape=out_shape, in_specs=[index, index, stay,...]
    unnamed x11 -> x13, local copies, waits for them, and re-layouts: 29.6 us -> 0.04 us
    all_to_all x0 -> x3, starting transfers between devices: none -> 17.1 us  [exchange(): return lax.all_to_all(rows, 'row', 0, 0)]
    reshape x4 -> x0, local copies, waits for them, and re-layouts: 13.1 us -> none  [the longest x2 6.54 us: operate(): own_forces = pick_rows(local_pick, current).reshape(blocks, NRHS, unknowns)]
    mul x2 -> x0, local copies, waits for them, and re-layouts: 7.74 us -> none  [operate(): jnp.einsum('kij,kri->krj', tiles, own_forces, preferred_element_type=jnp....]
    dot_general x2 -> x0, local copies, waits for them, and re-layouts: 7.71 us -> none  [operate(): jnp.einsum('kij,krj->kri', tiles, far_forces, preferred_element_type=jnp....]
  transfers between devices with their start and end apart: 4 -> 4, of which waited for: 3 -> 1; matrix products, arithmetic and copies ran while one was open for 57% -> 3% of each run, Pallas kernels for 0% -> 64%
where the time goes in v2:
time: 118 us; the launch traced here: 117 us
  Pallas kernels  74.9 us (63%)
  starting transfers between devices  17.1 us (14%)
  between operations  14.2 us (12%)
  matrix products  4.64 us (4%)
  waiting for transfers between devices  2.37 us (2%)
  other arithmetic  2.31 us (2%)
  local copies, waits for them, and re-layouts  1.39 us (1%)
    pallas_call x4, Pallas kernels, product_call(): pl.pallas_call(kernel, out_shape=out_shape, in_specs=[index, index, stay,...  53.2 us
    pallas_call x1, Pallas kernels, relay(): pl.pallas_call(relay_kernel, out_shape=pltpu.HBM((blocks // 2, 2 * unknow...  21.7 us
    all_to_all x3, starting transfers between devices, exchange(): return lax.all_to_all(rows, 'row', 0, 0)  17.1 us
  transfers between devices with their start and end apart: 4, of which 1 were waited for; matrix products, arithmetic and copies ran while one was open for 3% of the time, Pallas kernels for 64%

profile of v2, /device:TPU:0, one launch (start us, length us, event | category | flops | bytes accessed | tf_op | source)
XLA Modules:
  0.0 116.9 jit_solution(10349691039886978392)
XLA Ops:
  7.2 0.0 all-gather.3.cloned.1.call-start
  7.2 0.7 convert_element_type.39
  7.9 0.1 convert_element_type.40
  8.0 1.5 %fusion.6 = bf16[80,768]{1,0:T(8,128)(2,1)} fusion(bf16[1,256]{1,0:T(2,128)(2,1)S(1)} %convert_element_type.40, bf16[64,768]{1,0:T(8,128)(2,1)} %field_ref.1), kind=kLoop, calls=%fused_computation.12 | loop fusion | flops 368640 | bytes 221696 | tf_op jit(solution)/shard_map/concatenate | solution.py:290
  9.5 0.0 all-gather.3.cloned.1.call-update
  9.6 0.0 copy-start.2
  9.6 0.0 copy-start.3
  9.6 0.0 copy-start.5
  9.6 0.0 copy-start.1
  9.6 21.7 %relay.1.tile_ref = bf16[512,192,128]{2,1,0:T(8,128)(2,1)} custom-call(bf16[96,96,1024]{2,1,0:T(8,128)(2,1)} %bitcast.15), custom_call_target="tpu_custom_call" | custom-call | bytes 100663296 | tf_op jit(solution)/shard_map/relay/pallas_call | solution.py:73
  31.4 0.0 copy-start.4
  31.4 12.5 %mirror.2 = bf16[256,768]{1,0:T(8,128)(2,1)} custom-call(s32[1024]{0:T(1024)S(1)} %get-tuple-element.2.own_at, s32[1024]{0:T(1024)S(1)} %get-tuple-element.3.slot_at, bf16[512,192,128]{2,1,0:T(8,128)(2,1)} %relay.1.tile_ref, bf16[64,768]{1,0:T(8,128)(2,1)S(1)} %copy-done.1), custom_call_target="tpu_custom_call" | custom-call | flops 402653184 | bytes 25165824 | tf_op jit(solution)/shard_map/mirror/pallas_call | solution.py:176
  43.8 7.4 %all-to-all-start = ((bf16[16,16,768]{2,1,0:T(8,128)(2,1)}), bf16[16,16,768]{2,1,0:T(8,128)(2,1)S(1)}, u32[]{:S(2)}, u32[]{:S(2)}) async-start(bf16[16,16,768]{2,1,0:T(8,128)(2,1)} %bitcast.2), calls=%async_computation | async-start | bytes 786432 | tf_op jit(solution)/shard_map/all_to_all | solution.py:285
  51.3 0.1 squeeze.6
  51.3 0.1 add.35
  51.4 0.1 add.36
  51.5 2.3 %all-gather.3.cloned.1.call-done = bf16[1280,768]{1,0:T(8,128)(2,1)} async-done(((bf16[80,768]{1,0:T(8,128)(2,1)}), bf16[1280,768]{1,0:T(8,128)(2,1)}) %all-gather.3.cloned.1.call-update) | async-done | bytes 1966096 | tf_op jit(solution)/shard_map/all_gather | solution.py:290
  53.9 0.8 slice.4
  54.7 0.1 reshape_squeeze.3
  54.9 0.1 reshape.67
  55.0 2.3 %fusion.1.field_ref = bf16[256,768]{1,0:T(8,128)(2,1)S(1)} fusion(bf16[1280,768]{1,0:T(8,128)(2,1)} %all-gather.3.cloned.1.call-done, s32[256]{0:T(256)S(1)} %add.37), kind=kOutput, calls=%fused_computation.2 | convolution fusion | flops 503840768 | bytes 2360320 | tf_op jit(solution)/shard_map/dot_general | solution.py:314
  57.2 14.2 %direct.2 = f32[64,768]{1,0:T(8,128)S(1)} custom-call(s32[1024]{0:T(1024)S(1)} %copy-done.2, s32[1024]{0:T(1024)S(1)} %copy-done.3, bf16[512,192,128]{2,1,0:T(8,128)(2,1)} %relay.1.tile_ref, bf16[256,768]{1,0:T(8,128)(2,1)S(1)} %fusion.1.field_ref), custom_call_target="tpu_custom_call" | custom-call | flops 402653184 | bytes 25165824 | tf_op jit(solution)/shard_map/direct/pallas_call | solution.py:176
  71.4 0.0 all-to-all-done
  71.5 0.3 fusion.2.field_ref
  71.8 1.1 convolution_convert_fusion
  72.9 3.7 %all-to-all-start.1 = ((bf16[16,16,768]{2,1,0:T(8,128)(2,1)}), bf16[16,16,768]{2,1,0:T(8,128)(2,1)S(1)}, u32[]{:S(2)}, u32[]{:S(2)}) async-start(bf16[16,16,768]{2,1,0:T(8,128)(2,1)} %bitcast.4), calls=%async_computation.1 | async-start | bytes 786432 | tf_op jit(solution)/shard_map/all_to_all | solution.py:285
  76.5 12.3 %mirror.3 = bf16[256,768]{1,0:T(8,128)(2,1)} custom-call(s32[1024]{0:T(1024)S(1)} %get-tuple-element.2.own_at, s32[1024]{0:T(1024)S(1)} %get-tuple-element.3.slot_at, bf16[512,192,128]{2,1,0:T(8,128)(2,1)} %relay.1.tile_ref, bf16[64,768]{1,0:T(8,128)(2,1)S(1)} %fusion.2.field_ref), custom_call_target="tpu_custom_call" | custom-call | flops 402653184 | bytes 25165824 | tf_op jit(solution)/shard_map/mirror/pallas_call | solution.py:176
  88.9 0.0 all-to-all-done.1
  88.9 6.0 %all-to-all-start.2 = ((bf16[16,16,768]{2,1,0:T(8,128)(2,1)}), bf16[16,16,768]{2,1,0:T(8,128)(2,1)S(1)}, u32[]{:S(2)}, u32[]{:S(2)}) async-start(bf16[16,16,768]{2,1,0:T(8,128)(2,1)} %bitcast.6), calls=%async_computation.2 | async-start | bytes 786432 | tf_op jit(solution)/shard_map/all_to_all | solution.py:285
  94.9 14.2 %direct.3 = f32[64,768]{1,0:T(8,128)S(1)} custom-call(s32[1024]{0:T(1024)S(1)} %copy-done.2, s32[1024]{0:T(1024)S(1)} %copy-done.3, bf16[512,192,128]{2,1,0:T(8,128)(2,1)} %relay.1.tile_ref, bf16[256,768]{1,0:T(8,128)(2,1)S(1)} %bitcast.14), custom_call_target="tpu_custom_call" | custom-call | flops 402653184 | bytes 25165824 | tf_op jit(solution)/shard_map/direct/pallas_call | solution.py:176
  109.1 0.0 all-to-all-done.2
  109.1 0.9 fusion.3
  (12 shorter events, 0.1 us)
Async XLA Ops:
  7.2 46.7 %all-gather.3.cloned.1.call-start = ((), (), s32[]{:S(2)}) async-start(), calls=%async_computation.3 | async-start | bytes 2088960 | tf_op jit(solution)/shard_map/all_gather | solution.py:290
  9.6 21.8 %copy-start.2 = (s32[1024]{0:T(1024)S(1)}, s32[1024]{0:T(1024)}, u32[]{:S(2)}) copy-start(s32[1024]{0:T(1024)} %own_at.3) | copy-start | bytes 12292
  9.6 21.7 %copy-start.3 = (s32[1024]{0:T(1024)S(1)}, s32[1024]{0:T(1024)}, u32[]{:S(2)}) copy-start(s32[1024]{0:T(1024)} %slot_at.3) | copy-start | bytes 12292
  9.6 21.7 %copy-start.5 = (s32[1024]{0:T(1024)S(1)}, s32[1024]{0:T(1024)}, u32[]{:S(2)}) copy-start(s32[1024]{0:T(1024)} %param.10) | copy-start | bytes 12292
  9.6 21.7 %copy-start.1 = (bf16[64,768]{1,0:T(8,128)(2,1)S(1)}, bf16[64,768]{1,0:T(8,128)(2,1)}, u32[]{:S(2)}) copy-start(bf16[64,768]{1,0:T(8,128)(2,1)} %field_ref.1) | copy-start | bytes 294916
  31.4 19.9 %copy-start.4 = (s32[1,16,16]{2,1,0:T(8,128)S(1)}, s32[1,16,16]{2,1,0:T(8,128)}, u32[]{:S(2)}) copy-start(s32[1,16,16]{2,1,0:T(8,128)} %param.11) | copy-start | bytes 3076
  43.8 27.6 %all-to-all-start = ((bf16[16,16,768]{2,1,0:T(8,128)(2,1)}), bf16[16,16,768]{2,1,0:T(8,128)(2,1)S(1)}, u32[]{:S(2)}, u32[]{:S(2)}) async-start(bf16[16,16,768]{2,1,0:T(8,128)(2,1)} %bitcast.2), calls=%async_computation | async-start | bytes 786432 | tf_op jit(solution)/shard_map/all_to_all | solution.py:285
  71.8 17.1 %copy-start = (bf16[64,768]{1,0:T(8,128)(2,1)}, bf16[64,768]{1,0:T(8,128)(2,1)S(1)}, u32[]{:S(2)}) copy-start(bf16[64,768]{1,0:T(8,128)(2,1)S(1)} %fusion.2.field_ref) | copy-start | bytes 294916
  72.9 16.0 %all-to-all-start.1 = ((bf16[16,16,768]{2,1,0:T(8,128)(2,1)}), bf16[16,16,768]{2,1,0:T(8,128)(2,1)S(1)}, u32[]{:S(2)}, u32[]{:S(2)}) async-start(bf16[16,16,768]{2,1,0:T(8,128)(2,1)} %bitcast.4), calls=%async_computation.1 | async-start | bytes 786432 | tf_op jit(solution)/shard_map/all_to_all | solution.py:285
  88.9 20.2 %all-to-all-start.2 = ((bf16[16,16,768]{2,1,0:T(8,128)(2,1)}), bf16[16,16,768]{2,1,0:T(8,128)(2,1)S(1)}, u32[]{:S(2)}, u32[]{:S(2)}) async-start(bf16[16,16,768]{2,1,0:T(8,128)(2,1)} %bitcast.6), calls=%async_computation.2 | async-start | bytes 786432 | tf_op jit(solution)/shard_map/all_to_all | solution.py:285
Sparse Core Ops, SparseCore 0:
  10.3 43.5 all-gather.2

commit v3 on v2

--- a/solution.py
+++ b/solution.py
@@ -1,3 +1,5 @@
+import functools
+
 import jax
 import jax.numpy as jnp
 from jax import lax
@@ -7,18 +9,58 @@
 
 NRHS = 8
 LANES = 128
-QUADS_PER_LOOP = 16
-NOTE_ROWS = 16
+QUADS_PER_LOOP = 32
 PAIRS_PER_CHUNK = 64
-CHUNKS_HELD = 3
+CHUNKS_HELD = 4
 STRIDE_PAD = 1
 RELAY_LOOPS = 4
 TILE_BLOCK = 128
-RELAY_VMEM = 26 * 1024 * 1024
-PRODUCT_VMEM = 20 * 1024 * 1024
-
-
-def relay_kernel(native_ref, wide_ref, line_ref):
+RELAY_VMEM = 36 * 1024 * 1024
+PRODUCT_VMEM = 28 * 1024 * 1024
+
+
+def in_hbm(x):
+    return pltpu.with_memory_space_constraint(x, pltpu.HBM)
+
+
+def fill_near(field_ref, near_ref):
+    fibres, width = field_ref.shape
+    unknowns = width // NRHS
+    field = field_ref[...].astype(jnp.float32)
+    blank = jnp.zeros((fibres, unknowns), jnp.float32)
+    for r in range(NRHS):
+        part = field[:, r * unknowns : (r + 1) * unknowns]
+        near_ref[:fibres, r, :] = jnp.concatenate([part, blank], axis=1)
+        near_ref[fibres:, r, :] = jnp.concatenate([blank, part], axis=1)
+
+
+def mirror_quad(own_at, near_ref, first, halves):
+    fibres = near_ref.shape[0] // 2
+    left = jnp.concatenate(
+        [near_ref[own_at[first + t] + fibres * (t % 2)] for t in range(4)], axis=0
+    )
+    right = jnp.concatenate(halves, axis=1)
+    return jnp.dot(left.astype(jnp.bfloat16), right, preferred_element_type=jnp.float32)
+
+
+def mirror_add(slot_at, flag_at, sum_ref, first, found):
+    spare = sum_ref.shape[0] - 1
+    for t in range(4):
+        lane = (t // 2) * LANES
+        slot = jnp.where(flag_at[first + t] == 1, slot_at[first + t], spare)
+        sum_ref[slot] += found[t * NRHS : (t + 1) * NRHS, lane : lane + LANES]
+
+
+def slot_rows(sum_ref, slots, unknowns):
+    rows = [sum_ref[:slots, r, :][:, :unknowns] for r in range(NRHS)]
+    return jnp.concatenate(rows, axis=1)
+
+
+def relay_kernel(base, final, own_at, slot_at, flag_at, native_ref, field_ref, *rest):
+    if final:
+        _, sum_in_ref, wide_ref, slot_ref, line_ref, near_ref, sum_ref = rest
+    else:
+        wide_ref, sum_ref, line_ref, near_ref = rest
     step = pl.program_id(0)
     last = pl.num_programs(0) - 1
     unknowns = native_ref.shape[0]
@@ -29,7 +71,7 @@
     take_at = ((step + 1) % 2) * lines
     blank = jnp.zeros((LANES - unknowns, block), native_ref.dtype)
     rows = unknowns // RELAY_LOOPS
-    pairs = block // (2 * RELAY_LOOPS)
+    quads = block // (4 * RELAY_LOOPS)
 
     def turn(loop):
         for u in range(rows):
@@ -38,13 +80,23 @@
             line_ref[pl.ds(put_at + i * stride, block), :] = wide.T.astype(jnp.float32)
 
     def collect(loop):
-        for u in range(pairs):
-            pair = loop * pairs + u
-            for h in range(2):
-                lines_of = pl.ds(take_at + 2 * pair + h, unknowns, stride=stride)
-                wide_ref[pair, h * unknowns : (h + 1) * unknowns, :] = line_ref[
-                    lines_of, :
-                ].astype(wide_ref.dtype)
+        tile_at = (base + step - 1) * block
+        found = []
+        for u in range(quads):
+            pair = (loop * quads + u) * 2
+            halves = []
+            for p in range(2):
+                tiles = []
+                for h in range(2):
+                    lines_of = pl.ds(
+                        take_at + 2 * (pair + p) + h, unknowns, stride=stride
+                    )
+                    tiles.append(line_ref[lines_of, :].astype(wide_ref.dtype))
+                halves.append(jnp.concatenate(tiles, axis=0))
+                wide_ref[pair + p] = halves[p]
+            found.append(mirror_quad(own_at, near_ref, tile_at + 2 * pair, halves))
+        for u in range(quads):
+            mirror_add(slot_at, flag_at, sum_ref, tile_at + 4 * (loop * quads + u), found[u])
 
     def run(*parts):
         def body(loop, carry):
@@ -56,6 +108,11 @@
 
     @pl.when(step == 0)
     def _():
+        if final:
+            sum_ref[...] = sum_in_ref[...]
+        else:
+            sum_ref[...] = jnp.zeros_like(sum_ref)
+        fill_near(field_ref, near_ref)
         run(turn)
 
     @pl.when(jnp.logical_and(step > 0, step < last))
@@ -65,32 +122,68 @@
     @pl.when(step == last)
     def _():
         run(collect)
-
-
-def relay(native):
+        if final:
+            slot_ref[...] = slot_rows(sum_ref, slot_ref.shape[0], unknowns).astype(
+                slot_ref.dtype
+            )
+
+
+def relay_mirror(native, field, indices, slots, base, steps, earlier=None):
     unknowns, _, blocks = native.shape
-    steps = blocks // TILE_BLOCK
+    fibres, width = field.shape
+    final = earlier is not None
+    depth = 2 * unknowns
+    sum_shape = (slots + 1, NRHS, LANES)
+    in_specs = [
+        pl.BlockSpec(
+            (unknowns, unknowns, TILE_BLOCK),
+            lambda i, *_: (0, 0, base + jnp.minimum(i, steps - 1)),
+        ),
+        pl.BlockSpec((fibres, width), lambda i, *_: (0, 0)),
+    ]
+    operands = [in_hbm(native), in_hbm(field)]
+    out_shape = [pltpu.HBM((blocks // 2, depth, LANES), native.dtype)]
+    out_specs = [
+        pl.BlockSpec(
+            (TILE_BLOCK // 2, depth, LANES), lambda i, *_: (base + jnp.maximum(i - 1, 0), 0, 0)
+        )
+    ]
+    scratch_shapes = [
+        pltpu.VMEM((2 * unknowns * (TILE_BLOCK + STRIDE_PAD), LANES), jnp.float32),
+        pltpu.VMEM((2 * fibres, NRHS, depth), jnp.float32),
+    ]
+    if final:
+        wide, sums = earlier
+        in_specs += [
+            pl.BlockSpec(memory_space=pltpu.HBM),
+            pl.BlockSpec(sum_shape, lambda i, *_: (0, 0, 0)),
+        ]
+        operands += [in_hbm(wide), sums]
+        out_shape.append(jax.ShapeDtypeStruct((slots, width), jnp.bfloat16))
+        out_specs.append(pl.BlockSpec((slots, width), lambda i, *_: (0, 0)))
+        scratch_shapes.append(pltpu.VMEM(sum_shape, jnp.float32))
+    else:
+        out_shape.append(jax.ShapeDtypeStruct(sum_shape, jnp.float32))
+        out_specs.append(pl.BlockSpec(sum_shape, lambda i, *_: (0, 0, 0)))
     return pl.pallas_call(
-        relay_kernel,
-        out_shape=pltpu.HBM((blocks // 2, 2 * unknowns, LANES), native.dtype),
-        grid=(steps + 1,),
-        in_specs=[
-            pl.BlockSpec(
-                (unknowns, unknowns, TILE_BLOCK), lambda i: (0, 0, jnp.minimum(i, steps - 1))
-            )
-        ],
-        out_specs=pl.BlockSpec(
-            (TILE_BLOCK // 2, 2 * unknowns, LANES), lambda i: (jnp.maximum(i - 1, 0), 0, 0)
+        functools.partial(relay_kernel, base, final),
+        out_shape=out_shape,
+        grid_spec=pltpu.PrefetchScalarGridSpec(
+            num_scalar_prefetch=3,
+            grid=(steps + 1,),
+            in_specs=in_specs,
+            out_specs=out_specs,
+            scratch_shapes=scratch_shapes,
         ),
-        scratch_shapes=[
-            pltpu.VMEM((2 * unknowns * (TILE_BLOCK + STRIDE_PAD), LANES), jnp.float32)
-        ],
+        input_output_aliases={5: 0} if final else {},
         compiler_params=pltpu.CompilerParams(vmem_limit_bytes=RELAY_VMEM),
         cost_estimate=pl.CostEstimate(
-            flops=0, bytes_accessed=8 * blocks * unknowns * LANES, transcendentals=0
+            flops=4 * steps * TILE_BLOCK * unknowns * NRHS * LANES,
+            bytes_accessed=8 * steps * TILE_BLOCK * unknowns * LANES,
+            transcendentals=0,
         ),
-        name="relay",
-    )(pltpu.with_memory_space_constraint(native, pltpu.HBM))
+        name="relay_final" if final else "relay",
+    )(*[in_hbm(x) for x in indices], *operands)
 
 
 def chunk_copy(tile_ref, held_ref, ready, chunk):
@@ -129,42 +222,29 @@
 
 
 def mirror_kernel(
-    own_at, slot_at, tile_ref, field_ref, slot_ref, held_ref, ready, near_ref, sum_ref
+    own_at, slot_at, flag_at, tile_ref, field_ref, slot_ref, held_ref, ready, near_ref, sum_ref
 ):
     open_stream(tile_ref, held_ref, ready)
-    fibres, width = field_ref.shape
-    slots = slot_ref.shape[0]
-    unknowns = width // NRHS
+    slots, width = slot_ref.shape
     sum_ref[...] = jnp.zeros_like(sum_ref)
-    field = field_ref[...].astype(jnp.float32)
-    blank = jnp.zeros((fibres, unknowns), jnp.float32)
-    for r in range(NRHS):
-        part = field[:, r * unknowns : (r + 1) * unknowns]
-        near_ref[:fibres, r, :] = jnp.concatenate([part, blank], axis=1)
-        near_ref[fibres:, r, :] = jnp.concatenate([blank, part], axis=1)
+    fill_near(field_ref, near_ref)
 
     def quads(held, pair_at, chunk_at):
         first = 2 * (chunk_at + pair_at)
         found = []
         for u in range(QUADS_PER_LOOP):
             pair = pair_at + 2 * u
-            left = jnp.concatenate(
-                [near_ref[own_at[first + 4 * u + t]] for t in range(4)], axis=0
-            ).astype(jnp.bfloat16)
-            right = jnp.concatenate([held[pair], held[pair + 1]], axis=1)
-            found.append(jnp.dot(left, right, preferred_element_type=jnp.float32))
+            found.append(
+                mirror_quad(own_at, near_ref, first + 4 * u, [held[pair], held[pair + 1]])
+            )
         for u in range(QUADS_PER_LOOP):
-            for t in range(4):
-                lane = (t // 2) * LANES
-                slot = slot_at[first + 4 * u + t]
-                sum_ref[slot] += found[u][t * NRHS : (t + 1) * NRHS, lane : lane + LANES]
+            mirror_add(slot_at, flag_at, sum_ref, first + 4 * u, found[u])
 
     run_stream(tile_ref, held_ref, ready, quads)
-    rows = [sum_ref[:slots, r, :][:, :unknowns] for r in range(NRHS)]
-    slot_ref[...] = jnp.concatenate(rows, axis=1).astype(slot_ref.dtype)
-
-
-def product_call(kernel, name, tiles, field, own_at, slot_at, out_shape, scratch_shapes):
+    slot_ref[...] = slot_rows(sum_ref, slots, width // NRHS).astype(slot_ref.dtype)
+
+
+def product_call(kernel, name, tiles, field, indices, out_shape, scratch_shapes):
     pairs, depth, _ = tiles.shape
     whole = pl.BlockSpec(memory_space=pltpu.VMEM)
     stay = pl.BlockSpec(memory_space=pltpu.HBM)
@@ -176,7 +256,7 @@
     return pl.pallas_call(
         kernel,
         out_shape=out_shape,
-        in_specs=[index, index, stay, whole],
+        in_specs=[index] * len(indices) + [stay, whole],
         out_specs=whole,
         scratch_shapes=stream_shapes + scratch_shapes,
         compiler_params=pltpu.CompilerParams(vmem_limit_bytes=PRODUCT_VMEM),
@@ -186,18 +266,17 @@
             transcendentals=0,
         ),
         name=name,
-    )(own_at, slot_at, pltpu.with_memory_space_constraint(tiles, pltpu.HBM), field)
-
-
-def mirror(tiles, field, own_at, slot_at, slots):
+    )(*[in_hbm(x) for x in indices], in_hbm(tiles), field)
+
+
+def mirror(tiles, field, indices, slots):
     fibres, width = field.shape
     return product_call(
         mirror_kernel,
         "mirror",
         tiles,
         field,
-        own_at,
-        slot_at,
+        indices,
         jax.ShapeDtypeStruct((slots, width), jnp.bfloat16),
         [
             pltpu.VMEM((2 * fibres, NRHS, tiles.shape[1]), jnp.float32),
@@ -257,15 +336,14 @@
     own_ref[...] = jnp.concatenate(rows, axis=1)
 
 
-def direct(tiles, field, own_at, slot_at, fibres):
+def direct(tiles, field, indices, fibres):
     slots, width = field.shape
     return product_call(
         direct_kernel,
         "direct",
         tiles,
         field,
-        own_at,
-        slot_at,
+        indices,
         jax.ShapeDtypeStruct((fibres, width), jnp.float32),
         [
             pltpu.VMEM((slots, NRHS, LANES), jnp.float32),
@@ -284,18 +362,20 @@
     def exchange(rows):
         return lax.all_to_all(rows, "row", 0, 0)
 
-    me = lax.axis_index("row")
-    notes = want_list[0].astype(jnp.bfloat16).reshape(1, slots)
-    notes = jnp.pad(notes, ((0, NOTE_ROWS - 1), (0, row_width - slots)))
-    everyone = lax.all_gather(jnp.concatenate([forces, notes], axis=0), "row")
-    wanted = everyone[:, fibres, :slots].reshape(peers, peers, capacity)
-    asked = lax.dynamic_index_in_dim(wanted, me, 1, False).astype(jnp.int32).reshape(slots)
+    direct_at = (tile_local, tile_slot)
+    mirror_at = (tile_local, tile_slot, tile_flag)
+    half = blocks // TILE_BLOCK // 2
+    relay_part = functools.partial(
+        relay_mirror, tiles.transpose(1, 2, 0), forces, mirror_at, slots
+    )
+
+    asked = exchange(want_list[0])
+    part = relay_part(0, half)
+    asked, part = lax.optimization_barrier((asked, part))
+    asked = asked.reshape(slots)
     asked_pick = (asked[:, None] == jnp.arange(fibres, dtype=jnp.int32)[None, :]).astype(
         jnp.bfloat16
     )
-    mirror_own = tile_local + fibres * (jnp.arange(blocks, dtype=jnp.int32) % 2)
-    mirror_slot = jnp.where(tile_flag == 1, tile_slot, slots)
-
     def fetch(current):
         rows = jnp.dot(asked_pick, current, preferred_element_type=jnp.float32)
         rows = rows.astype(jnp.bfloat16).reshape(peers, capacity, row_width)
@@ -307,20 +387,14 @@
             asked_pick, back, (((0,), (0,)), ((), ())), preferred_element_type=jnp.float32
         )
 
-    wide = relay(tiles.transpose(1, 2, 0))
-    rows = (jnp.arange(peers, dtype=jnp.int32)[:, None] * (fibres + NOTE_ROWS) + want_list[0]).reshape(slots)
-    spread = jnp.arange(peers * (fibres + NOTE_ROWS), dtype=jnp.int32)
-    first_pick = (rows[:, None] == spread[None, :]).astype(jnp.bfloat16)
-    far = jnp.dot(
-        first_pick, everyone.reshape(-1, row_width), preferred_element_type=jnp.float32
-    ).astype(jnp.bfloat16)
-    slot_part = mirror(wide, forces, mirror_own, mirror_slot, slots)
-    own_part = direct(wide, far, tile_local, tile_slot, fibres)
+    far = fetch(forces)
+    wide, slot_part = relay_part(half, blocks // TILE_BLOCK - half, part)
+    own_part = direct(wide, far, direct_at, fibres)
     krylov_one = (own_part + give_back(slot_part)).astype(jnp.bfloat16)
 
     far = fetch(krylov_one)
-    slot_part = mirror(wide, krylov_one, mirror_own, mirror_slot, slots)
-    own_part = direct(wide, far, tile_local, tile_slot, fibres)
+    slot_part = mirror(wide, krylov_one, mirror_at, slots)
+    own_part = direct(wide, far, direct_at, fibres)
     krylov_two = (own_part + give_back(slot_part)).astype(jnp.bfloat16)
     return (krylov_one, krylov_two)
 

time: 118 us -> 103 us (0.87)
  starting transfers between devices: 17.1 us -> 30.9 us
  between operations: 14.2 us -> 0.72 us
  Pallas kernels: 74.9 us -> 65.6 us
  other arithmetic: 2.31 us -> 0 us
  waiting for transfers between devices: 2.37 us -> 0.53 us
  local copies, waits for them, and re-layouts: 1.39 us -> 0.08 us
    all_to_all x3 -> x5, starting transfers between devices: 17.1 us -> 30.9 us  [exchange(): return lax.all_to_all(rows, 'row', 0, 0)]
    pallas_call x5, Pallas kernels: 74.9 us -> 65.6 us  [the longest x3 38.2 us: product_call(): pl.pallas_call(kernel, out_shape=out_shape, in_specs=[index] * len(indice...]
    all_gather x1 -> x0, waiting for transfers between devices: 2.34 us -> none  [per_device(): everyone = lax.all_gather(jnp.concatenate([forces, notes], axis=0), 'row')]
    dot_general x1 -> x0, matrix products: 2.28 us -> none  [per_device(): jnp.dot(first_pick, everyone.reshape(-1, row_width), preferred_element_ty...]
    dot_general x1 -> x2, matrix products: 1.1 us -> 3.07 us  [fetch(): rows = jnp.dot(asked_pick, current, preferred_element_type=jnp.float32)]
    concatenate x1 -> x0, other arithmetic: 1.55 us -> none  [per_device(): everyone = lax.all_gather(jnp.concatenate([forces, notes], axis=0), 'row')]
  transfers between devices with their start and end apart: 4 -> 5, of which waited for: 1 -> 1; matrix products, arithmetic and copies ran while one was open for 3% -> 0% of each run, Pallas kernels for 64% -> 64%
where the time goes in v3:
time: 103 us; the launch traced here: 102 us
  Pallas kernels  65.6 us (64%)
  starting transfers between devices  30.9 us (30%)
  matrix products  4.32 us (4%)
    pallas_call x3, Pallas kernels, product_call(): pl.pallas_call(kernel, out_shape=out_shape, in_specs=[index] * len(indice...  38.2 us
    all_to_all x5, starting transfers between devices, exchange(): return lax.all_to_all(rows, 'row', 0, 0)  30.9 us
    pallas_call x2, Pallas kernels, relay_mirror(): pl.pallas_call(functools.partial(relay_kernel, base, final), out_shape=ou...  27.3 us
    dot_general x2, matrix products, fetch(): rows = jnp.dot(asked_pick, current, preferred_element_type=jnp.float32)  3.07 us
  transfers between devices with their start and end apart: 5, of which 1 were waited for; matrix products, arithmetic and copies ran while one was open for 0% of the time, Pallas kernels for 64%

profile of v3, /device:TPU:0, one launch (start us, length us, event | category | flops | bytes accessed | tf_op | source)
XLA Modules:
  0.0 102.1 jit_solution(2378158649583779588)
XLA Ops:
  0.6 7.4 %all-to-all-start = ((s32[16,1,16]{2,1,0:T(1,128)}), s32[16,1,16]{2,1,0:T(1,128)S(1)}, u32[]{:S(2)}, u32[]{:S(2)}) async-start(s32[16,1,16]{2,1,0:T(1,128)} %bitcast.22), calls=%async_computation | async-start | bytes 16384 | tf_op jit(solution)/shard_map/all_to_all | solution.py:363
  8.0 13.2 %relay.1 = (bf16[512,192,128]{2,1,0:T(8,128)(2,1)}, f32[257,8,128]{2,1,0:T(8,128)S(1)}) custom-call(s32[1024]{0:T(1024)} %own_at.9, s32[1024]{0:T(1024)} %slot_at.9, s32[1024]{0:T(1024)} %flag_at.5, bf16[96,96,1024]{2,1,0:T(8,128)(2,1)} %bitcast.17, bf16[64,768]{1,0:T(8,128)(2,1)} %field_ref.3), custom_call_target="tpu_custom_call" | custom-call | flops 201326592 | bytes 50331648 | tf_op jit(solution)/shard_map/relay/pallas_call | solution.py:168
  21.3 0.0 all-to-all-done
  21.3 0.1 eq.15
  21.4 2.0 %convolution_convert_fusion.1 = bf16[256,768]{1,0:T(8,128)(2,1)} fusion(bf16[64,768]{1,0:T(8,128)(2,1)} %field_ref.3, s32[256]{0:T(256)S(1)} %eq.15), kind=kOutput, calls=%fused_computation.1 | convolution fusion | flops 25378816 | bytes 492544 | tf_op jit(solution)/shard_map/dot_general | solution.py:380
  23.3 6.0 %all-to-all-start.1 = ((bf16[16,16,768]{2,1,0:T(8,128)(2,1)}), bf16[16,16,768]{2,1,0:T(8,128)(2,1)S(1)}, u32[]{:S(2)}, u32[]{:S(2)}) async-start(bf16[16,16,768]{2,1,0:T(8,128)(2,1)} %bitcast.3), calls=%async_computation.1 | async-start | bytes 786432 | tf_op jit(solution)/shard_map/all_to_all | solution.py:363
  29.4 14.1 %relay_final.1 = (bf16[512,192,128]{2,1,0:T(8,128)(2,1)}, bf16[256,768]{1,0:T(8,128)(2,1)}) custom-call(s32[1024]{0:T(1024)} %own_at.9, s32[1024]{0:T(1024)} %slot_at.9, s32[1024]{0:T(1024)} %flag_at.5, bf16[96,96,1024]{2,1,0:T(8,128)(2,1)} %bitcast.18, bf16[64,768]{1,0:T(8,128)(2,1)} %field_ref.3, ...), custom_call_target="tpu_custom_call", output_to_operand_aliasing={{0}: (5, {})} | custom-call | flops 201326592 | bytes 50331648 | tf_op jit(solution)/shard_map/relay_final/pallas_call | solution.py:168
  43.4 0.0 all-to-all-done.1
  43.5 6.0 %all-to-all-start.2 = ((bf16[16,16,768]{2,1,0:T(8,128)(2,1)}), bf16[16,16,768]{2,1,0:T(8,128)(2,1)S(1)}, u32[]{:S(2)}, u32[]{:S(2)}) async-start(bf16[16,16,768]{2,1,0:T(8,128)(2,1)} %bitcast.5), calls=%async_computation.2 | async-start | bytes 786432 | tf_op jit(solution)/shard_map/all_to_all | solution.py:363
  49.5 13.3 %direct.2 = f32[64,768]{1,0:T(8,128)S(1)} custom-call(s32[1024]{0:T(1024)} %own_at.9, s32[1024]{0:T(1024)} %slot_at.9, bf16[512,192,128]{2,1,0:T(8,128)(2,1)} %get-tuple-element.13.tile_ref, bf16[256,768]{1,0:T(8,128)(2,1)S(1)} %bitcast.15), custom_call_target="tpu_custom_call" | custom-call | flops 402653184 | bytes 25165824 | tf_op jit(solution)/shard_map/direct/pallas_call | solution.py:256
  62.8 0.0 all-to-all-done.2
  62.8 0.3 fusion.field_ref
  63.1 0.0 copy-start
  63.1 1.1 %convolution_convert_fusion = bf16[256,768]{1,0:T(8,128)(2,1)} fusion(bf16[64,768]{1,0:T(8,128)(2,1)S(1)} %fusion.field_ref, s32[256]{0:T(256)S(1)} %eq.15), kind=kOutput, calls=%fused_computation | convolution fusion | flops 25378816 | bytes 492544 | tf_op jit(solution)/shard_map/dot_general | solution.py:380
  64.2 6.0 %all-to-all-start.3 = ((bf16[16,16,768]{2,1,0:T(8,128)(2,1)}), bf16[16,16,768]{2,1,0:T(8,128)(2,1)S(1)}, u32[]{:S(2)}, u32[]{:S(2)}) async-start(bf16[16,16,768]{2,1,0:T(8,128)(2,1)} %bitcast.7), calls=%async_computation.3 | async-start | bytes 786432 | tf_op jit(solution)/shard_map/all_to_all | solution.py:363
  70.2 11.7 %mirror.1 = bf16[256,768]{1,0:T(8,128)(2,1)} custom-call(s32[1024]{0:T(1024)} %own_at.9, s32[1024]{0:T(1024)} %slot_at.9, s32[1024]{0:T(1024)} %flag_at.5, bf16[512,192,128]{2,1,0:T(8,128)(2,1)} %get-tuple-element.13.tile_ref, bf16[64,768]{1,0:T(8,128)(2,1)S(1)} %fusion.field_ref), custom_call_target="tpu_custom_call" | custom-call | flops 402653184 | bytes 25165824 | tf_op jit(solution)/shard_map/mirror/pallas_call | solution.py:256
  81.8 0.5 all-to-all-done.3
  82.4 5.5 %all-to-all-start.4 = ((bf16[16,16,768]{2,1,0:T(8,128)(2,1)}), bf16[16,16,768]{2,1,0:T(8,128)(2,1)S(1)}, u32[]{:S(2)}, u32[]{:S(2)}) async-start(bf16[16,16,768]{2,1,0:T(8,128)(2,1)} %bitcast.9), calls=%async_computation.4 | async-start | bytes 786432 | tf_op jit(solution)/shard_map/all_to_all | solution.py:363
  87.9 13.3 %direct.3 = f32[64,768]{1,0:T(8,128)S(1)} custom-call(s32[1024]{0:T(1024)} %own_at.9, s32[1024]{0:T(1024)} %slot_at.9, bf16[512,192,128]{2,1,0:T(8,128)(2,1)} %get-tuple-element.13.tile_ref, bf16[256,768]{1,0:T(8,128)(2,1)S(1)} %bitcast.16), custom_call_target="tpu_custom_call" | custom-call | flops 402653184 | bytes 25165824 | tf_op jit(solution)/shard_map/direct/pallas_call | solution.py:256
  101.2 0.0 copy-done
  101.2 0.0 all-to-all-done.4
  101.2 0.9 fusion.1
Async XLA Ops:
  0.6 20.7 %all-to-all-start = ((s32[16,1,16]{2,1,0:T(1,128)}), s32[16,1,16]{2,1,0:T(1,128)S(1)}, u32[]{:S(2)}, u32[]{:S(2)}) async-start(s32[16,1,16]{2,1,0:T(1,128)} %bitcast.22), calls=%async_computation | async-start | bytes 16384 | tf_op jit(solution)/shard_map/all_to_all | solution.py:363
  23.3 20.1 %all-to-all-start.1 = ((bf16[16,16,768]{2,1,0:T(8,128)(2,1)}), bf16[16,16,768]{2,1,0:T(8,128)(2,1)S(1)}, u32[]{:S(2)}, u32[]{:S(2)}) async-start(bf16[16,16,768]{2,1,0:T(8,128)(2,1)} %bitcast.3), calls=%async_computation.1 | async-start | bytes 786432 | tf_op jit(solution)/shard_map/all_to_all | solution.py:363
  43.5 19.3 %all-to-all-start.2 = ((bf16[16,16,768]{2,1,0:T(8,128)(2,1)}), bf16[16,16,768]{2,1,0:T(8,128)(2,1)S(1)}, u32[]{:S(2)}, u32[]{:S(2)}) async-start(bf16[16,16,768]{2,1,0:T(8,128)(2,1)} %bitcast.5), calls=%async_computation.2 | async-start | bytes 786432 | tf_op jit(solution)/shard_map/all_to_all | solution.py:363
  63.1 38.1 %copy-start = (bf16[64,768]{1,0:T(8,128)(2,1)}, bf16[64,768]{1,0:T(8,128)(2,1)S(1)}, u32[]{:S(2)}) copy-start(bf16[64,768]{1,0:T(8,128)(2,1)S(1)} %fusion.field_ref) | copy-start | bytes 294916
  64.2 18.2 %all-to-all-start.3 = ((bf16[16,16,768]{2,1,0:T(8,128)(2,1)}), bf16[16,16,768]{2,1,0:T(8,128)(2,1)S(1)}, u32[]{:S(2)}, u32[]{:S(2)}) async-start(bf16[16,16,768]{2,1,0:T(8,128)(2,1)} %bitcast.7), calls=%async_computation.3 | async-start | bytes 786432 | tf_op jit(solution)/shard_map/all_to_all | solution.py:363
  82.4 18.8 %all-to-all-start.4 = ((bf16[16,16,768]{2,1,0:T(8,128)(2,1)}), bf16[16,16,768]{2,1,0:T(8,128)(2,1)S(1)}, u32[]{:S(2)}, u32[]{:S(2)}) async-start(bf16[16,16,768]{2,1,0:T(8,128)(2,1)} %bitcast.9), calls=%async_computation.4 | async-start | bytes 786432 | tf_op jit(solution)/shard_map/all_to_all | solution.py:363

commit v4 on v3

v4 whole, which is shorter than its diff:
```python
import functools

import jax
import jax.numpy as jnp
from jax import lax
from jax.experimental import pallas as pl
from jax.experimental.pallas import tpu as pltpu
from jax.sharding import PartitionSpec as P

NRHS = 8
LANES = 128
SHARES = 3
HOSTS = SHARES + 1
CHUNKS_HELD = 3
RELAY_LOOPS = 4
STRIDE_PAD = 1
RELAY_VMEM = 52 * 1024 * 1024
PRODUCT_VMEM = 36 * 1024 * 1024
PAIRS_PER_CHUNK = LANES // 2


def in_hbm(x):
    return pltpu.with_memory_space_constraint(x, pltpu.HBM)


def tiles_of(chunk):
    group, share = chunk // SHARES, chunk % SHARES
    return share, (group * HOSTS + share) * LANES, (group * HOSTS + SHARES) * LANES


def lane_window(shape, start, stop):
    lane = lax.broadcasted_iota(jnp.int32, shape, len(shape) - 1)
    return jnp.logical_and(lane >= start, lane < stop)


def fill_near(field_ref, near_ref):
    fibres, width = field_ref.shape
    unknowns = width // NRHS
    field = field_ref[...].astype(jnp.float32)
    blank = jnp.zeros((fibres, unknowns), jnp.float32)
    for r in range(NRHS):
        part = field[:, r * unknowns : (r + 1) * unknowns]
        near_ref[:fibres, r, :] = jnp.concatenate([part, blank], axis=1)
        near_ref[fibres:, r, :] = jnp.concatenate([blank, part], axis=1)


def mirror_quad(own_at, near_ref, chunk, pair, halves):
    fibres = near_ref.shape[0] // 2
    _, host_at, guest_at = tiles_of(chunk)
    left = []
    for t in range(4):
        for first in (host_at, guest_at):
            left.append(near_ref[own_at[first + 2 * pair + t] + fibres * (t % 2)])
    left = jnp.concatenate(left, axis=0).astype(jnp.bfloat16)
    right = jnp.concatenate(halves, axis=1)
    return jnp.dot(left, right, preferred_element_type=jnp.float32)


def mirror_add(slot_at, flag_at, sums, chunk, pair, found):
    rows = sums[0].shape[0]
    share, host_at, guest_at = tiles_of(chunk)
    for t in range(4):
        lane = (t // 2) * LANES
        for m, first in enumerate((host_at, guest_at)):
            tile = first + 2 * pair + t
            slot = jnp.where(flag_at[tile] == 1, slot_at[tile], rows - 1)
            if m == 1:
                slot = slot + share * rows
            group = (2 * t + m) * NRHS
            sums[2 * m + t % 2][slot] += found[group : group + NRHS, lane : lane + LANES]


def clear(refs):
    for ref in refs:
        ref[...] = jnp.zeros_like(ref)


def write_slots(sums, slot_ref, before_ref=None):
    slots, width = slot_ref.shape
    unknowns = width // NRHS
    piece = unknowns // SHARES
    rows = sums[0].shape[0]
    step = 32

    def both(pair, at):
        total = pair[0][pl.ds(at, step)] + pair[1][pl.ds(at, step)]
        return total.reshape(step * NRHS, LANES)

    def gather(loop, carry):
        at = loop * step
        total = both(sums[:2], at)
        for share in range(SHARES):
            part = both(sums[2:], share * rows + at)
            part = pltpu.roll(part, (share * piece - unknowns) % LANES, 1)
            here = lane_window(part.shape, share * piece, (share + 1) * piece)
            total = total + jnp.where(here, part, 0.0)
        sums[0][pl.ds(at, step)] = total.reshape(step, NRHS, LANES)
        return carry

    lax.fori_loop(0, slots // step, gather, 0, unroll=2)
    parts = [sums[0][:slots, r, :][:, :unknowns] for r in range(NRHS)]
    total = jnp.concatenate(parts, axis=1)
    if before_ref is not None:
        total = total + before_ref[...]
    slot_ref[...] = total.astype(slot_ref.dtype)


def sum_scratch(slots):
    return [pltpu.VMEM((n * (slots + 1), NRHS, LANES), jnp.float32) for n in (1, 1, SHARES, SHARES)]


def relay_kernel(base, final, own_at, slot_at, flag_at, host_ref, guest_ref, field_ref, *rest):
    before_ref = rest[1] if final else None
    wide_ref, slot_ref, line_ref, near_ref, *sums = rest[2:] if final else rest
    step = pl.program_id(0)
    last = pl.num_programs(0) - 1
    unknowns = host_ref.shape[0]
    stride = LANES + STRIDE_PAD
    lines = unknowns * stride
    put_at = (step % 2) * lines
    take_at = ((step + 1) % 2) * lines
    rows = unknowns // RELAY_LOOPS
    quads = PAIRS_PER_CHUNK // (2 * RELAY_LOOPS)

    def turn(loop):
        for u in range(rows):
            i = loop * rows + u
            block = jnp.concatenate([host_ref[i], guest_ref[i]], axis=0)
            line_ref[pl.ds(put_at + i * stride, LANES), :] = block.T.astype(jnp.float32)

    def collect(loop):
        found = []
        for u in range(quads):
            pair = (loop * quads + u) * 2
            halves = []
            for p in range(2):
                tiles = []
                for h in range(2):
                    lines_of = pl.ds(take_at + 2 * (pair + p) + h, unknowns, stride=stride)
                    tiles.append(line_ref[lines_of, :].astype(wide_ref.dtype))
                halves.append(jnp.concatenate(tiles, axis=0))
                wide_ref[pair + p] = halves[p]
            found.append(mirror_quad(own_at, near_ref, base + step - 1, pair, halves))
        for u in range(quads):
            pair = (loop * quads + u) * 2
            mirror_add(slot_at, flag_at, sums, base + step - 1, pair, found[u])

    def run(*parts):
        def body(loop, carry):
            for part in parts:
                part(loop)
            return carry

        lax.fori_loop(0, RELAY_LOOPS, body, 0)

    @pl.when(step == 0)
    def _():
        clear(sums)
        fill_near(field_ref, near_ref)
        run(turn)

    @pl.when(jnp.logical_and(step > 0, step < last))
    def _():
        run(collect, turn)

    @pl.when(step == last)
    def _():
        run(collect)
        write_slots(sums, slot_ref, before_ref)


def relay_mirror(native, field, indices, slots, base, count, earlier=None):
    unknowns, _, blocks = native.shape
    fibres, width = field.shape
    depth = 2 * unknowns
    chunks = blocks // (HOSTS * LANES) * SHARES
    piece = unknowns // SHARES
    final = earlier is not None

    def host_map(i, *_):
        _, host_at, _ = tiles_of(base + jnp.minimum(i, count - 1))
        return (0, 0, host_at // LANES)

    def guest_map(i, *_):
        share, _, guest_at = tiles_of(base + jnp.minimum(i, count - 1))
        return (0, share, guest_at // LANES)

    in_specs = [
        pl.BlockSpec((unknowns, unknowns, LANES), host_map),
        pl.BlockSpec((unknowns, piece, LANES), guest_map),
        pl.BlockSpec((fibres, width), lambda i, *_: (0, 0)),
    ]
    operands = [in_hbm(x) for x in (*indices, native, native, field)]
    if final:
        in_specs.append(pl.BlockSpec(memory_space=pltpu.HBM))
        in_specs.append(pl.BlockSpec((slots, width), lambda i, *_: (0, 0)))
        operands += [in_hbm(x) for x in earlier]
    return pl.pallas_call(
        functools.partial(relay_kernel, base, final),
        out_shape=[
            pltpu.HBM((chunks * PAIRS_PER_CHUNK, depth, LANES), native.dtype),
            jax.ShapeDtypeStruct((slots, width), jnp.bfloat16 if final else jnp.float32),
        ],
        grid_spec=pltpu.PrefetchScalarGridSpec(
            num_scalar_prefetch=3,
            grid=(count + 1,),
            in_specs=in_specs,
            out_specs=[
                pl.BlockSpec(
                    (PAIRS_PER_CHUNK, depth, LANES), lambda i, *_: (base + jnp.maximum(i - 1, 0), 0, 0)
                ),
                pl.BlockSpec((slots, width), lambda i, *_: (0, 0)),
            ],
            scratch_shapes=[
                pltpu.VMEM((2 * unknowns * (LANES + STRIDE_PAD), LANES), jnp.float32),
                pltpu.VMEM((2 * fibres, NRHS, depth), jnp.float32),
            ]
            + sum_scratch(slots),
        ),
        input_output_aliases={6: 0} if final else {},
        compiler_params=pltpu.CompilerParams(vmem_limit_bytes=RELAY_VMEM),
        cost_estimate=pl.CostEstimate(
            flops=16 * count * LANES * unknowns * NRHS * LANES,
            bytes_accessed=4 * count * LANES * unknowns * LANES,
            transcendentals=0,
        ),
        name="relay_rest" if final else "relay",
    )(*operands)


def chunk_copy(tile_ref, held_ref, ready, chunk):
    slot = chunk % CHUNKS_HELD
    return pltpu.make_async_copy(
        tile_ref.at[pl.ds(chunk * PAIRS_PER_CHUNK, PAIRS_PER_CHUNK)],
        held_ref.at[slot],
        ready.at[slot],
    )


def open_stream(tile_ref, held_ref, ready):
    for chunk in range(CHUNKS_HELD - 1):
        chunk_copy(tile_ref, held_ref, ready, chunk).start()


def run_stream(tile_ref, held_ref, ready, product):
    chunks = tile_ref.shape[0] // PAIRS_PER_CHUNK

    def body(chunk, carry):
        chunk_copy(tile_ref, held_ref, ready, chunk).wait()

        @pl.when(chunk + CHUNKS_HELD - 1 < chunks)
        def _():
            chunk_copy(tile_ref, held_ref, ready, chunk + CHUNKS_HELD - 1).start()

        product(held_ref.at[chunk % CHUNKS_HELD], chunk)
        return carry

    lax.fori_loop(0, chunks, body, 0)


def mirror_kernel(
    own_at,
    slot_at,
    flag_at,
    tile_ref,
    field_ref,
    slot_ref,
    held_ref,
    ready,
    near_ref,
    *sums,
):
    open_stream(tile_ref, held_ref, ready)
    clear(sums)
    fill_near(field_ref, near_ref)

    def product(held, chunk):
        pairs = range(0, PAIRS_PER_CHUNK, 2)
        found = [
            mirror_quad(own_at, near_ref, chunk, pair, [held[pair], held[pair + 1]])
            for pair in pairs
        ]
        for pair, one in zip(pairs, found):
            mirror_add(slot_at, flag_at, sums, chunk, pair, one)

    run_stream(tile_ref, held_ref, ready, product)
    write_slots(sums, slot_ref)


def product_call(kernel, name, tiles, field, indices, out_shape, scratch_shapes):
    pairs, depth, _ = tiles.shape
    whole = pl.BlockSpec(memory_space=pltpu.VMEM)
    stay = pl.BlockSpec(memory_space=pltpu.HBM)
    stream_shapes = [
        pltpu.VMEM((CHUNKS_HELD, PAIRS_PER_CHUNK, depth, LANES), tiles.dtype),
        pltpu.SemaphoreType.DMA((CHUNKS_HELD,)),
    ]
    index = pl.BlockSpec(memory_space=pltpu.SMEM)
    return pl.pallas_call(
        kernel,
        out_shape=out_shape,
        in_specs=[index] * len(indices) + [stay, whole],
        out_specs=whole,
        scratch_shapes=stream_shapes + scratch_shapes,
        compiler_params=pltpu.CompilerParams(vmem_limit_bytes=PRODUCT_VMEM),
        cost_estimate=pl.CostEstimate(
            flops=4 * pairs * depth * NRHS * LANES,
            bytes_accessed=2 * pairs * depth * LANES,
            transcendentals=0,
        ),
        name=name,
    )(*[in_hbm(x) for x in indices], in_hbm(tiles), field)


def mirror(tiles, field, indices, slots):
    fibres, width = field.shape
    return product_call(
        mirror_kernel,
        "mirror",
        tiles,
        field,
        indices,
        jax.ShapeDtypeStruct((slots, width), jnp.bfloat16),
        [
            pltpu.VMEM((2 * fibres, NRHS, tiles.shape[1]), jnp.float32),
        ]
        + sum_scratch(slots),
    )


def fill_far(field_ref, far_ref):
    slots, width = field_ref.shape
    unknowns = width // NRHS
    piece = unknowns // SHARES
    step = 32
    field = field_ref[...].astype(jnp.float32)
    blank = jnp.zeros((slots, LANES - unknowns), jnp.float32)
    for r in range(NRHS):
        part = field[:, r * unknowns : (r + 1) * unknowns]
        far_ref[:slots, r, :] = jnp.concatenate([part, blank], axis=1)

    def spread(loop, carry):
        at = loop * step
        whole = far_ref[pl.ds(at, step)].reshape(step * NRHS, LANES)
        there = lane_window(whole.shape, unknowns, LANES)
        for share in range(SHARES):
            part = pltpu.roll(whole, (unknowns - share * piece) % LANES, 1)
            part = jnp.where(there, part, 0.0)
            far_ref[pl.ds((1 + share) * slots + at, step)] = part.reshape(step, NRHS, LANES)
        return carry

    lax.fori_loop(0, slots // step, spread, 0)


def direct_kernel(
    own_at, slot_at, tile_ref, field_ref, own_ref, held_ref, ready, far_ref, *sums
):
    open_stream(tile_ref, held_ref, ready)
    slots, width = field_ref.shape
    unknowns = width // NRHS
    clear(sums)
    fill_far(field_ref, far_ref)
    none = [jnp.zeros((NRHS, LANES), jnp.float32)] * 4

    def product(held, chunk):
        share, host_at, guest_at = tiles_of(chunk)
        pairs = range(0, PAIRS_PER_CHUNK, 2)
        found = []
        for pair in pairs:
            far = []
            for t in range(4):
                far.append(far_ref[slot_at[host_at + 2 * pair + t]])
                far.append(far_ref[slot_at[guest_at + 2 * pair + t] + (1 + share) * slots])
            left = jnp.concatenate(
                [
                    jnp.concatenate(far[:4] + none, axis=0),
                    jnp.concatenate(none + far[4:], axis=0),
                ],
                axis=1,
            ).astype(jnp.bfloat16)
            right = jnp.concatenate([held[pair], held[pair + 1]], axis=1)
            found.append(
                lax.dot_general(
                    left, right, (((1,), (1,)), ((), ())), preferred_element_type=jnp.float32
                )
            )
        for pair, one in zip(pairs, found):
            for t in range(4):
                for m, first in enumerate((host_at, guest_at)):
                    rows = one[(2 * t + m) * NRHS : (2 * t + m + 1) * NRHS]
                    own = own_at[first + 2 * pair + t]
                    if t % 2 == 0:
                        sums[m][own] += rows[:, :LANES]
                    else:
                        sums[2 + m][own] += rows

    run_stream(tile_ref, held_ref, ready, product)
    rows = [
        (sums[0][:, r, :] + sums[1][:, r, :])[:, :unknowns]
        + (sums[2][:, r, :] + sums[3][:, r, :])[:, unknowns:]
        for r in range(NRHS)
    ]
    own_ref[...] = jnp.concatenate(rows, axis=1)


def direct(tiles, field, indices, fibres):
    slots, width = field.shape
    return product_call(
        direct_kernel,
        "direct",
        tiles,
        field,
        indices,
        jax.ShapeDtypeStruct((fibres, width), jnp.float32),
        [
            pltpu.VMEM((HOSTS * slots, NRHS, LANES), jnp.float32),
            pltpu.VMEM((fibres, NRHS, LANES), jnp.float32),
            pltpu.VMEM((fibres, NRHS, LANES), jnp.float32),
            pltpu.VMEM((fibres, NRHS, tiles.shape[1]), jnp.float32),
            pltpu.VMEM((fibres, NRHS, tiles.shape[1]), jnp.float32),
        ],
    )


def per_device(forces, tiles, tile_local, tile_slot, tile_flag, want_list):
    fibres, row_width = forces.shape
    _, peers, capacity = want_list.shape
    slots = peers * capacity

    def exchange(rows):
        return lax.all_to_all(rows, "row", 0, 0, tiled=True)

    direct_at = (tile_local, tile_slot)
    mirror_at = (tile_local, tile_slot, tile_flag)
    chunks = tiles.shape[0] // (HOSTS * LANES) * SHARES
    relay_part = functools.partial(
        relay_mirror, tiles.transpose(1, 2, 0), forces, mirror_at, slots
    )

    asked = exchange(want_list[0])
    part = relay_part(0, chunks // 2)
    asked, part = lax.optimization_barrier((asked, part))
    asked = asked.reshape(slots)
    asked_pick = (asked[:, None] == jnp.arange(fibres, dtype=jnp.int32)[None, :]).astype(
        jnp.bfloat16
    )
    def fetch(current):
        rows = jnp.dot(asked_pick, current, preferred_element_type=jnp.float32)
        return exchange(rows.astype(jnp.bfloat16))

    def give_back(slot_part):
        return lax.dot_general(
            asked_pick, exchange(slot_part), (((0,), (0,)), ((), ())), preferred_element_type=jnp.float32
        )

    far = fetch(forces)
    wide, slot_part = relay_part(chunks // 2, chunks - chunks // 2, part)
    own_part = direct(wide, far, direct_at, fibres)
    krylov_one = (own_part + give_back(slot_part)).astype(jnp.bfloat16)

    far = fetch(krylov_one)
    slot_part = mirror(wide, krylov_one, mirror_at, slots)
    own_part = direct(wide, far, direct_at, fibres)
    krylov_two = (own_part + give_back(slot_part)).astype(jnp.bfloat16)
    return (krylov_one, krylov_two)


def solution(mesh):
    spec = ("groups", "row")
    in_specs = (
        P(spec, None),
        P(spec, None, None),
        P(spec),
        P(spec),
        P(spec),
        P(spec, None, None),
    )
    out_specs = (P(spec, None), P(spec, None))
    return jax.shard_map(
        per_device, mesh=mesh, in_specs=in_specs, out_specs=out_specs, check_vma=False
    )
```

time: 103 us -> 99.8 us (0.969)
  Pallas kernels: 65.6 us -> 61.8 us
    pallas_call x3, Pallas kernels: 38.2 us -> 35.1 us  [product_call(): pl.pallas_call(kernel, out_shape=out_shape, in_specs=[index] * len(indice...]
  transfers between devices with their start and end apart: 5 -> 5, of which waited for: 1 -> 2; matrix products, arithmetic and copies ran while one was open for 0% -> 0% of each run, Pallas kernels for 64% -> 62%
where the time goes in v4:
time: 99.8 us; the launch traced here: 99.1 us
  Pallas kernels  61.8 us (62%)
  starting transfers between devices  30.7 us (31%)
  matrix products  3.4 us (3%)
  waiting for transfers between devices  1.49 us (1%)
    pallas_call x3, Pallas kernels, product_call(): pl.pallas_call(kernel, out_shape=out_shape, in_specs=[index] * len(indice...  35.1 us
    all_to_all x5, starting transfers between devices, exchange(): return lax.all_to_all(rows, 'row', 0, 0, tiled=True)  30.7 us
    pallas_call x2, Pallas kernels, relay_mirror(): pl.pallas_call(functools.partial(relay_kernel, base, final), out_shape=[p...  26.7 us
    dot_general x2, matrix products, fetch(): rows = jnp.dot(asked_pick, current, preferred_element_type=jnp.float32)  2.15 us
  transfers between devices with their start and end apart: 5, of which 2 were waited for; matrix products, arithmetic and copies ran while one was open for 0% of the time, Pallas kernels for 62%

profile of v4, /device:TPU:0, one launch (start us, length us, event | category | flops | bytes accessed | tf_op | source)
XLA Modules:
  0.0 99.1 jit_solution(10790736473581601273)
XLA Ops:
  0.6 7.4 %all-to-all-start = ((s32[16,1,16]{2,1,0:T(1,128)}), s32[16,1,16]{2,1,0:T(1,128)S(1)}, u32[]{:S(2)}, u32[]{:S(2)}) async-start(s32[16,1,16]{2,1,0:T(1,128)} %bitcast.24), calls=%async_computation | async-start | bytes 16384 | tf_op jit(solution)/shard_map/all_to_all | solution.py:431
  8.0 0.0 copy-start.2
  8.0 13.2 %relay.1 = (bf16[384,192,128]{2,1,0:T(8,128)(2,1)}, f32[256,768]{1,0:T(8,128)S(1)}) custom-call(s32[1024]{0:T(1024)} %own_at.9, s32[1024]{0:T(1024)} %slot_at.9, s32[1024]{0:T(1024)} %flag_at.5, bf16[96,96,1024]{2,1,0:T(8,128)(2,1)} %bitcast.17, bf16[96,96,1024]{2,1,0:T(8,128)(2,1)} %bitcast.18, bf16[64,768]{1,0:T(8,128)(2,1)} %field_ref.3), custom_call_target="tpu_custom_call" | custom-call | flops 603979776 | bytes 18874368 | tf_op jit(solution)/shard_map/relay/pallas_call | solution.py:198
  21.3 0.0 copy-start.1
  21.3 0.9 copy-done.1
  22.2 0.0 all-to-all-done
  22.2 0.1 eq.15
  22.3 0.0 copy-done.2
  22.3 1.1 %convolution_convert_fusion.1 = bf16[256,768]{1,0:T(8,128)(2,1)} fusion(bf16[64,768]{1,0:T(8,128)(2,1)S(1)} %copy-done.2, s32[256]{0:T(256)S(1)} %eq.15), kind=kOutput, calls=%fused_computation.1 | convolution fusion | flops 25378816 | bytes 492544 | tf_op jit(solution)/shard_map/dot_general | solution.py:448
  23.4 6.0 %all-to-all-start.1 = ((bf16[16,16,768]{2,1,0:T(8,128)(2,1)}), bf16[16,16,768]{2,1,0:T(8,128)(2,1)S(1)}, u32[]{:S(2)}, u32[]{:S(2)}) async-start(bf16[16,16,768]{2,1,0:T(8,128)(2,1)} %bitcast.3), calls=%async_computation.1 | async-start | bytes 786432 | tf_op jit(solution)/shard_map/all_to_all | solution.py:431
  29.4 13.5 %relay_rest.1 = (bf16[384,192,128]{2,1,0:T(8,128)(2,1)}, bf16[256,768]{1,0:T(8,128)(2,1)}) custom-call(s32[1024]{0:T(1024)} %own_at.9, s32[1024]{0:T(1024)} %slot_at.9, s32[1024]{0:T(1024)} %flag_at.5, bf16[96,96,1024]{2,1,0:T(8,128)(2,1)} %bitcast.19, bf16[96,96,1024]{2,1,0:T(8,128)(2,1)} %bitcast.20, ...), custom_call_target="tpu_custom_call", output_to_operand_aliasing={{0}: (6, {})} | custom-call | flops 603979776 | bytes 18874368 | tf_op jit(solution)/shard_map/relay_rest/pallas_call | solution.py:198
  42.8 0.0 all-to-all-done.1
  42.9 6.0 %all-to-all-start.2 = ((bf16[16,16,768]{2,1,0:T(8,128)(2,1)}), bf16[16,16,768]{2,1,0:T(8,128)(2,1)S(1)}, u32[]{:S(2)}, u32[]{:S(2)}) async-start(bf16[16,16,768]{2,1,0:T(8,128)(2,1)} %bitcast.5), calls=%async_computation.2 | async-start | bytes 786432 | tf_op jit(solution)/shard_map/all_to_all | solution.py:431
  48.9 11.4 %direct.2 = f32[64,768]{1,0:T(8,128)S(1)} custom-call(s32[1024]{0:T(1024)} %own_at.9, s32[1024]{0:T(1024)} %slot_at.9, bf16[384,192,128]{2,1,0:T(8,128)(2,1)} %get-tuple-element.13.tile_ref, bf16[256,768]{1,0:T(8,128)(2,1)S(1)} %bitcast.15), custom_call_target="tpu_custom_call" | custom-call | flops 301989888 | bytes 18874368 | tf_op jit(solution)/shard_map/direct/pallas_call | solution.py:299
  60.3 0.7 all-to-all-done.2
  61.1 0.3 fusion.field_ref
  61.4 0.0 copy-start
  61.4 1.1 %convolution_convert_fusion = bf16[256,768]{1,0:T(8,128)(2,1)} fusion(bf16[64,768]{1,0:T(8,128)(2,1)S(1)} %fusion.field_ref, s32[256]{0:T(256)S(1)} %eq.15), kind=kOutput, calls=%fused_computation | convolution fusion | flops 25378816 | bytes 492544 | tf_op jit(solution)/shard_map/dot_general | solution.py:448
  62.4 5.3 %all-to-all-start.3 = ((bf16[16,16,768]{2,1,0:T(8,128)(2,1)}), bf16[16,16,768]{2,1,0:T(8,128)(2,1)S(1)}, u32[]{:S(2)}, u32[]{:S(2)}) async-start(bf16[16,16,768]{2,1,0:T(8,128)(2,1)} %bitcast.7), calls=%async_computation.3 | async-start | bytes 786432 | tf_op jit(solution)/shard_map/all_to_all | solution.py:431
  67.7 12.2 %mirror.1 = bf16[256,768]{1,0:T(8,128)(2,1)} custom-call(s32[1024]{0:T(1024)} %own_at.9, s32[1024]{0:T(1024)} %slot_at.9, s32[1024]{0:T(1024)} %flag_at.5, bf16[384,192,128]{2,1,0:T(8,128)(2,1)} %get-tuple-element.13.tile_ref, bf16[64,768]{1,0:T(8,128)(2,1)S(1)} %fusion.field_ref), custom_call_target="tpu_custom_call" | custom-call | flops 301989888 | bytes 18874368 | tf_op jit(solution)/shard_map/mirror/pallas_call | solution.py:299
  79.9 0.0 all-to-all-done.3
  79.9 6.0 %all-to-all-start.4 = ((bf16[16,16,768]{2,1,0:T(8,128)(2,1)}), bf16[16,16,768]{2,1,0:T(8,128)(2,1)S(1)}, u32[]{:S(2)}, u32[]{:S(2)}) async-start(bf16[16,16,768]{2,1,0:T(8,128)(2,1)} %bitcast.9), calls=%async_computation.4 | async-start | bytes 786432 | tf_op jit(solution)/shard_map/all_to_all | solution.py:431
  85.9 11.4 %direct.3 = f32[64,768]{1,0:T(8,128)S(1)} custom-call(s32[1024]{0:T(1024)} %own_at.9, s32[1024]{0:T(1024)} %slot_at.9, bf16[384,192,128]{2,1,0:T(8,128)(2,1)} %get-tuple-element.13.tile_ref, bf16[256,768]{1,0:T(8,128)(2,1)S(1)} %bitcast.16), custom_call_target="tpu_custom_call" | custom-call | flops 301989888 | bytes 18874368 | tf_op jit(solution)/shard_map/direct/pallas_call | solution.py:299
  97.4 0.0 copy-done
  97.4 0.7 all-to-all-done.4
  98.1 0.9 fusion.1
Async XLA Ops:
  0.6 21.6 %all-to-all-start = ((s32[16,1,16]{2,1,0:T(1,128)}), s32[16,1,16]{2,1,0:T(1,128)S(1)}, u32[]{:S(2)}, u32[]{:S(2)}) async-start(s32[16,1,16]{2,1,0:T(1,128)} %bitcast.24), calls=%async_computation | async-start | bytes 16384 | tf_op jit(solution)/shard_map/all_to_all | solution.py:431
  8.0 14.2 %copy-start.2 = (bf16[64,768]{1,0:T(8,128)(2,1)S(1)}, bf16[64,768]{1,0:T(8,128)(2,1)}, u32[]{:S(2)}) copy-start(bf16[64,768]{1,0:T(8,128)(2,1)} %field_ref.3) | copy-start | bytes 294916
  21.3 0.9 copy-start.1
  23.4 19.5 %all-to-all-start.1 = ((bf16[16,16,768]{2,1,0:T(8,128)(2,1)}), bf16[16,16,768]{2,1,0:T(8,128)(2,1)S(1)}, u32[]{:S(2)}, u32[]{:S(2)}) async-start(bf16[16,16,768]{2,1,0:T(8,128)(2,1)} %bitcast.3), calls=%async_computation.1 | async-start | bytes 786432 | tf_op jit(solution)/shard_map/all_to_all | solution.py:431
  42.9 18.2 %all-to-all-start.2 = ((bf16[16,16,768]{2,1,0:T(8,128)(2,1)}), bf16[16,16,768]{2,1,0:T(8,128)(2,1)S(1)}, u32[]{:S(2)}, u32[]{:S(2)}) async-start(bf16[16,16,768]{2,1,0:T(8,128)(2,1)} %bitcast.5), calls=%async_computation.2 | async-start | bytes 786432 | tf_op jit(solution)/shard_map/all_to_all | solution.py:431
  61.4 36.0 %copy-start = (bf16[64,768]{1,0:T(8,128)(2,1)}, bf16[64,768]{1,0:T(8,128)(2,1)S(1)}, u32[]{:S(2)}) copy-start(bf16[64,768]{1,0:T(8,128)(2,1)S(1)} %fusion.field_ref) | copy-start | bytes 294916
  62.4 17.5 %all-to-all-start.3 = ((bf16[16,16,768]{2,1,0:T(8,128)(2,1)}), bf16[16,16,768]{2,1,0:T(8,128)(2,1)S(1)}, u32[]{:S(2)}, u32[]{:S(2)}) async-start(bf16[16,16,768]{2,1,0:T(8,128)(2,1)} %bitcast.7), calls=%async_computation.3 | async-start | bytes 786432 | tf_op jit(solution)/shard_map/all_to_all | solution.py:431
  79.9 18.2 %all-to-all-start.4 = ((bf16[16,16,768]{2,1,0:T(8,128)(2,1)}), bf16[16,16,768]{2,1,0:T(8,128)(2,1)S(1)}, u32[]{:S(2)}, u32[]{:S(2)}) async-start(bf16[16,16,768]{2,1,0:T(8,128)(2,1)} %bitcast.9), calls=%async_computation.4 | async-start | bytes 786432 | tf_op jit(solution)/shard_map/all_to_all | solution.py:431

commit v5 on v4

--- a/solution.py
+++ b/solution.py
@@ -109,26 +109,66 @@
     return [pltpu.VMEM((n * (slots + 1), NRHS, LANES), jnp.float32) for n in (1, 1, SHARES, SHARES)]
 
 
-def relay_kernel(base, final, own_at, slot_at, flag_at, host_ref, guest_ref, field_ref, *rest):
-    before_ref = rest[1] if final else None
-    wide_ref, slot_ref, line_ref, near_ref, *sums = rest[2:] if final else rest
-    step = pl.program_id(0)
-    last = pl.num_programs(0) - 1
-    unknowns = host_ref.shape[0]
+def relay_kernel(base, count, final, own_at, slot_at, flag_at, native_ref, field_ref, *rest):
+    if final:
+        _, before_at, wide_ref, slot_ref, *rest = rest
+        rest, before_ref = rest[:-1], rest[-1]
+    else:
+        before_at, before_ref = None, None
+        wide_ref, slot_ref, *rest = rest
+    if not final:
+        echo_ref, *rest = rest
+    host_ref, guest_ref, made_ref, near_from_ref, line_ref, near_ref, ready, *sums = rest
+    unknowns = native_ref.shape[0]
+    piece = unknowns // SHARES
     stride = LANES + STRIDE_PAD
     lines = unknowns * stride
-    put_at = (step % 2) * lines
-    take_at = ((step + 1) % 2) * lines
     rows = unknowns // RELAY_LOOPS
     quads = PAIRS_PER_CHUNK // (2 * RELAY_LOOPS)
 
-    def turn(loop):
+    def loads(n):
+        share, host_at, guest_at = tiles_of(base + n)
+        slot = n % 2
+        return (
+            pltpu.make_async_copy(
+                native_ref.at[:, :, pl.ds(host_at, LANES)], host_ref.at[slot], ready.at[slot]
+            ),
+            pltpu.make_async_copy(
+                native_ref.at[:, pl.ds(share * piece, piece), pl.ds(guest_at, LANES)],
+                guest_ref.at[slot],
+                ready.at[2 + slot],
+            ),
+        )
+
+    def store(n):
+        return pltpu.make_async_copy(
+            made_ref.at[n % 2],
+            wide_ref.at[pl.ds((base + n) * PAIRS_PER_CHUNK, PAIRS_PER_CHUNK)],
+            ready.at[4 + n % 2],
+        )
+
+    fetch_field = pltpu.make_async_copy(field_ref, near_from_ref, ready.at[6])
+    fetch_field.start()
+    for n in range(min(2, count)):
+        for copy in loads(n):
+            copy.start()
+    if final:
+        fetch_before = pltpu.make_async_copy(before_at, before_ref, ready.at[7])
+        fetch_before.start()
+    clear(sums)
+    fetch_field.wait()
+    if not final:
+        echo_ref[...] = near_from_ref[...]
+    fill_near(near_from_ref, near_ref)
+
+    def turn(n, loop):
         for u in range(rows):
             i = loop * rows + u
-            block = jnp.concatenate([host_ref[i], guest_ref[i]], axis=0)
-            line_ref[pl.ds(put_at + i * stride, LANES), :] = block.T.astype(jnp.float32)
-
-    def collect(loop):
+            block = jnp.concatenate([host_ref[n % 2, i], guest_ref[n % 2, i]], axis=0)
+            at = (n % 2) * lines + i * stride
+            line_ref[pl.ds(at, LANES), :] = block.T.astype(jnp.float32)
+
+    def collect(n, loop):
         found = []
         for u in range(quads):
             pair = (loop * quads + u) * 2
@@ -136,37 +176,42 @@
             for p in range(2):
                 tiles = []
                 for h in range(2):
-                    lines_of = pl.ds(take_at + 2 * (pair + p) + h, unknowns, stride=stride)
-                    tiles.append(line_ref[lines_of, :].astype(wide_ref.dtype))
+                    at = (n % 2) * lines + 2 * (pair + p) + h
+                    lines_of = pl.ds(at, unknowns, stride=stride)
+                    tiles.append(line_ref[lines_of, :].astype(made_ref.dtype))
                 halves.append(jnp.concatenate(tiles, axis=0))
-                wide_ref[pair + p] = halves[p]
-            found.append(mirror_quad(own_at, near_ref, base + step - 1, pair, halves))
+                made_ref[n % 2, pair + p] = halves[p]
+            found.append(mirror_quad(own_at, near_ref, base + n, pair, halves))
         for u in range(quads):
             pair = (loop * quads + u) * 2
-            mirror_add(slot_at, flag_at, sums, base + step - 1, pair, found[u])
-
-    def run(*parts):
-        def body(loop, carry):
-            for part in parts:
-                part(loop)
+            mirror_add(slot_at, flag_at, sums, base + n, pair, found[u])
+
+    for n in range(count + 1):
+        if n < count:
+            for copy in loads(n):
+                copy.wait()
+        if n >= 3:
+            store(n - 3).wait()
+
+        def body(loop, carry, n=n):
+            if n >= 1:
+                collect(n - 1, loop)
+            if n < count:
+                turn(n, loop)
             return carry
 
         lax.fori_loop(0, RELAY_LOOPS, body, 0)
-
-    @pl.when(step == 0)
-    def _():
-        clear(sums)
-        fill_near(field_ref, near_ref)
-        run(turn)
-
-    @pl.when(jnp.logical_and(step > 0, step < last))
-    def _():
-        run(collect, turn)
-
-    @pl.when(step == last)
-    def _():
-        run(collect)
-        write_slots(sums, slot_ref, before_ref)
+        if n + 2 < count:
+            for copy in loads(n + 2):
+                copy.start()
+        if n >= 1:
+            store(n - 1).start()
+
+    if final:
+        fetch_before.wait()
+    write_slots(sums, slot_ref, before_ref)
+    for n in range(max(count - 2, 0), count):
+        store(n).wait()
 
 
 def relay_mirror(native, field, indices, slots, base, count, earlier=None):
@@ -174,50 +219,36 @@
     fibres, width = field.shape
     depth = 2 * unknowns
     chunks = blocks // (HOSTS * LANES) * SHARES
-    piece = unknowns // SHARES
     final = earlier is not None
-
-    def host_map(i, *_):
-        _, host_at, _ = tiles_of(base + jnp.minimum(i, count - 1))
-        return (0, 0, host_at // LANES)
-
-    def guest_map(i, *_):
-        share, _, guest_at = tiles_of(base + jnp.minimum(i, count - 1))
-        return (0, share, guest_at // LANES)
-
-    in_specs = [
-        pl.BlockSpec((unknowns, unknowns, LANES), host_map),
-        pl.BlockSpec((unknowns, piece, LANES), guest_map),
-        pl.BlockSpec((fibres, width), lambda i, *_: (0, 0)),
-    ]
-    operands = [in_hbm(x) for x in (*indices, native, native, field)]
+    whole = pl.BlockSpec(memory_space=pltpu.VMEM)
+    stay = pl.BlockSpec(memory_space=pltpu.HBM)
+    index = pl.BlockSpec(memory_space=pltpu.SMEM)
+    operands = [in_hbm(x) for x in (*indices, native, field)]
+    out_shape = [pltpu.HBM((chunks * PAIRS_PER_CHUNK, depth, LANES), native.dtype)]
     if final:
-        in_specs.append(pl.BlockSpec(memory_space=pltpu.HBM))
-        in_specs.append(pl.BlockSpec((slots, width), lambda i, *_: (0, 0)))
         operands += [in_hbm(x) for x in earlier]
+        out_shape.append(jax.ShapeDtypeStruct((slots, width), jnp.bfloat16))
+    else:
+        out_shape.append(jax.ShapeDtypeStruct((slots, width), jnp.float32))
+        out_shape.append(pltpu.VMEM((fibres, width), field.dtype))
+    scratch_shapes = [
+        pltpu.VMEM((2, unknowns, unknowns, LANES), native.dtype),
+        pltpu.VMEM((2, unknowns, unknowns // SHARES, LANES), native.dtype),
+        pltpu.VMEM((2, PAIRS_PER_CHUNK, depth, LANES), native.dtype),
+        pltpu.VMEM((fibres, width), field.dtype),
+        pltpu.VMEM((2 * unknowns * (LANES + STRIDE_PAD), LANES), jnp.float32),
+        pltpu.VMEM((2 * fibres, NRHS, depth), jnp.float32),
+        pltpu.SemaphoreType.DMA((8,)),
+    ] + sum_scratch(slots)
+    if final:
+        scratch_shapes.append(pltpu.VMEM((slots, width), jnp.float32))
     return pl.pallas_call(
-        functools.partial(relay_kernel, base, final),
-        out_shape=[
-            pltpu.HBM((chunks * PAIRS_PER_CHUNK, depth, LANES), native.dtype),
-            jax.ShapeDtypeStruct((slots, width), jnp.bfloat16 if final else jnp.float32),
-        ],
-        grid_spec=pltpu.PrefetchScalarGridSpec(
-            num_scalar_prefetch=3,
-            grid=(count + 1,),
-            in_specs=in_specs,
-            out_specs=[
-                pl.BlockSpec(
-                    (PAIRS_PER_CHUNK, depth, LANES), lambda i, *_: (base + jnp.maximum(i - 1, 0), 0, 0)
-                ),
-                pl.BlockSpec((slots, width), lambda i, *_: (0, 0)),
-            ],
-            scratch_shapes=[
-                pltpu.VMEM((2 * unknowns * (LANES + STRIDE_PAD), LANES), jnp.float32),
-                pltpu.VMEM((2 * fibres, NRHS, depth), jnp.float32),
-            ]
-            + sum_scratch(slots),
-        ),
-        input_output_aliases={6: 0} if final else {},
+        functools.partial(relay_kernel, base, count, final),
+        out_shape=out_shape,
+        in_specs=[index] * len(indices) + [stay] * (len(operands) - len(indices)),
+        out_specs=[stay] + [whole] * (len(out_shape) - 1),
+        scratch_shapes=scratch_shapes,
+        input_output_aliases={5: 0} if final else {},
         compiler_params=pltpu.CompilerParams(vmem_limit_bytes=RELAY_VMEM),
         cost_estimate=pl.CostEstimate(
             flops=16 * count * LANES * unknowns * NRHS * LANES,
@@ -438,8 +469,8 @@
     )
 
     asked = exchange(want_list[0])
-    part = relay_part(0, chunks // 2)
-    asked, part = lax.optimization_barrier((asked, part))
+    *part, echo = relay_part(0, chunks // 2)
+    asked, part, echo = lax.optimization_barrier((asked, part, echo))
     asked = asked.reshape(slots)
     asked_pick = (asked[:, None] == jnp.arange(fibres, dtype=jnp.int32)[None, :]).astype(
         jnp.bfloat16
@@ -453,7 +484,7 @@
             asked_pick, exchange(slot_part), (((0,), (0,)), ((), ())), preferred_element_type=jnp.float32
         )
 
-    far = fetch(forces)
+    far = fetch(echo)
     wide, slot_part = relay_part(chunks // 2, chunks - chunks // 2, part)
     own_part = direct(wide, far, direct_at, fibres)
     krylov_one = (own_part + give_back(slot_part)).astype(jnp.bfloat16)

time: 99.8 us -> 94.3 us (0.945)
  Pallas kernels: 61.8 us -> 56.3 us
  starting transfers between devices: 30.7 us -> 29.5 us
  waiting for transfers between devices: 1.49 us -> 2.68 us
    pallas_call x2, Pallas kernels: 26.7 us -> 21.2 us  [relay_mirror(): pl.pallas_call(functools.partial(relay_kernel, base, count, final), out_s...]
    all_to_all x5, waiting for transfers between devices: 1.49 us -> 2.68 us  [exchange(): return lax.all_to_all(rows, 'row', 0, 0, tiled=True)]
    all_to_all x5, starting transfers between devices: 30.7 us -> 29.5 us  [exchange(): return lax.all_to_all(rows, 'row', 0, 0, tiled=True)]
  transfers between devices with their start and end apart: 5 -> 5, of which waited for: 2 -> 3; matrix products, arithmetic and copies ran while one was open for 0% -> 0% of each run, Pallas kernels for 62% -> 60%
where the time goes in v5:
time: 94.3 us; the launch traced here: 93.6 us
  Pallas kernels  56.3 us (60%)
  starting transfers between devices  29.5 us (31%)
  matrix products  3.41 us (4%)
  waiting for transfers between devices  2.68 us (3%)
  local copies, waits for them, and re-layouts  0.97 us (1%)
    pallas_call x3, Pallas kernels, product_call(): pl.pallas_call(kernel, out_shape=out_shape, in_specs=[index] * len(indice...  35.1 us
    all_to_all x5, starting transfers between devices, exchange(): return lax.all_to_all(rows, 'row', 0, 0, tiled=True)  29.5 us
    pallas_call x2, Pallas kernels, relay_mirror(): pl.pallas_call(functools.partial(relay_kernel, base, count, final), out_s...  21.2 us
    all_to_all x5, waiting for transfers between devices, exchange(): return lax.all_to_all(rows, 'row', 0, 0, tiled=True)  2.68 us
    dot_general x2, matrix products, fetch(): rows = jnp.dot(asked_pick, current, preferred_element_type=jnp.float32)  2.17 us
  transfers between devices with their start and end apart: 5, of which 3 were waited for; matrix products, arithmetic and copies ran while one was open for 0% of the time, Pallas kernels for 60%

profile of v5, /device:TPU:0, one launch (start us, length us, event | category | flops | bytes accessed | tf_op | source)
XLA Modules:
  0.0 93.6 jit_solution(966887287625033352)
XLA Ops:
  0.6 7.4 %all-to-all-start = ((s32[16,1,16]{2,1,0:T(1,128)}), s32[16,1,16]{2,1,0:T(1,128)S(1)}, u32[]{:S(2)}, u32[]{:S(2)}) async-start(s32[16,1,16]{2,1,0:T(1,128)} %bitcast.22), calls=%async_computation | async-start | bytes 16384 | tf_op jit(solution)/shard_map/all_to_all | solution.py:462
  8.0 10.2 %relay.1 = (bf16[384,192,128]{2,1,0:T(8,128)(2,1)}, f32[256,768]{1,0:T(8,128)S(1)}, bf16[64,768]{1,0:T(8,128)(2,1)S(1)}) custom-call(s32[1024]{0:T(1024)} %own_at.9, s32[1024]{0:T(1024)} %slot_at.9, s32[1024]{0:T(1024)} %flag_at.5, bf16[96,96,1024]{2,1,0:T(8,128)(2,1)} %bitcast.17, bf16[64,768]{1,0:T(8,128)(2,1)} %field_ref.3), custom_call_target="tpu_custom_call" | custom-call | flops 603979776 | bytes 18874368 | tf_op jit(solution)/shard_map/relay/pallas_call | solution.py:245
  18.2 0.0 copy-start.1
  18.2 0.9 copy-done.1
  19.1 0.0 all-to-all-done
  19.1 0.1 eq.15
  19.2 1.1 %convolution_convert_fusion.1 = bf16[256,768]{1,0:T(8,128)(2,1)} fusion(bf16[64,768]{1,0:T(8,128)(2,1)S(1)} %get-tuple-element.18, s32[256]{0:T(256)S(1)} %eq.15), kind=kOutput, calls=%fused_computation.1 | convolution fusion | flops 25378816 | bytes 492544 | tf_op jit(solution)/shard_map/dot_general | solution.py:479
  20.3 6.0 %all-to-all-start.1 = ((bf16[16,16,768]{2,1,0:T(8,128)(2,1)}), bf16[16,16,768]{2,1,0:T(8,128)(2,1)S(1)}, u32[]{:S(2)}, u32[]{:S(2)}) async-start(bf16[16,16,768]{2,1,0:T(8,128)(2,1)} %bitcast.3), calls=%async_computation.1 | async-start | bytes 786432 | tf_op jit(solution)/shard_map/all_to_all | solution.py:462
  26.3 11.0 %relay_rest.1 = (bf16[384,192,128]{2,1,0:T(8,128)(2,1)}, bf16[256,768]{1,0:T(8,128)(2,1)}) custom-call(s32[1024]{0:T(1024)} %own_at.9, s32[1024]{0:T(1024)} %slot_at.9, s32[1024]{0:T(1024)} %flag_at.5, bf16[96,96,1024]{2,1,0:T(8,128)(2,1)} %bitcast.18, bf16[64,768]{1,0:T(8,128)(2,1)} %field_ref.3, ...), custom_call_target="tpu_custom_call", output_to_operand_aliasing={{0}: (5, {})} | custom-call | flops 603979776 | bytes 18874368 | tf_op jit(solution)/shard_map/relay_rest/pallas_call | solution.py:245
  37.3 1.2 %all-to-all-done.1 = bf16[16,16,768]{2,1,0:T(8,128)(2,1)S(1)} async-done(((bf16[16,16,768]{2,1,0:T(8,128)(2,1)}), bf16[16,16,768]{2,1,0:T(8,128)(2,1)S(1)}, u32[]{:S(2)}, u32[]{:S(2)}) %all-to-all-start.1) | async-done | bytes 393248 | tf_op jit(solution)/shard_map/all_to_all | solution.py:462
  38.5 4.9 %all-to-all-start.2 = ((bf16[16,16,768]{2,1,0:T(8,128)(2,1)}), bf16[16,16,768]{2,1,0:T(8,128)(2,1)S(1)}, u32[]{:S(2)}, u32[]{:S(2)}) async-start(bf16[16,16,768]{2,1,0:T(8,128)(2,1)} %bitcast.5), calls=%async_computation.2 | async-start | bytes 786432 | tf_op jit(solution)/shard_map/all_to_all | solution.py:462
  43.4 11.4 %direct.2 = f32[64,768]{1,0:T(8,128)S(1)} custom-call(s32[1024]{0:T(1024)} %own_at.9, s32[1024]{0:T(1024)} %slot_at.9, bf16[384,192,128]{2,1,0:T(8,128)(2,1)} %get-tuple-element.16.tile_ref, bf16[256,768]{1,0:T(8,128)(2,1)S(1)} %bitcast.15), custom_call_target="tpu_custom_call" | custom-call | flops 301989888 | bytes 18874368 | tf_op jit(solution)/shard_map/direct/pallas_call | solution.py:330
  54.8 0.7 all-to-all-done.2
  55.6 0.3 fusion.field_ref
  55.9 0.0 copy-start
  55.9 1.1 %convolution_convert_fusion = bf16[256,768]{1,0:T(8,128)(2,1)} fusion(bf16[64,768]{1,0:T(8,128)(2,1)S(1)} %fusion.field_ref, s32[256]{0:T(256)S(1)} %eq.15), kind=kOutput, calls=%fused_computation | convolution fusion | flops 25378816 | bytes 492544 | tf_op jit(solution)/shard_map/dot_general | solution.py:479
  57.0 5.3 %all-to-all-start.3 = ((bf16[16,16,768]{2,1,0:T(8,128)(2,1)}), bf16[16,16,768]{2,1,0:T(8,128)(2,1)S(1)}, u32[]{:S(2)}, u32[]{:S(2)}) async-start(bf16[16,16,768]{2,1,0:T(8,128)(2,1)} %bitcast.7), calls=%async_computation.3 | async-start | bytes 786432 | tf_op jit(solution)/shard_map/all_to_all | solution.py:462
  62.2 12.2 %mirror.1 = bf16[256,768]{1,0:T(8,128)(2,1)} custom-call(s32[1024]{0:T(1024)} %own_at.9, s32[1024]{0:T(1024)} %slot_at.9, s32[1024]{0:T(1024)} %flag_at.5, bf16[384,192,128]{2,1,0:T(8,128)(2,1)} %get-tuple-element.16.tile_ref, bf16[64,768]{1,0:T(8,128)(2,1)S(1)} %fusion.field_ref), custom_call_target="tpu_custom_call" | custom-call | flops 301989888 | bytes 18874368 | tf_op jit(solution)/shard_map/mirror/pallas_call | solution.py:330
  74.4 0.0 all-to-all-done.3
  74.4 6.0 %all-to-all-start.4 = ((bf16[16,16,768]{2,1,0:T(8,128)(2,1)}), bf16[16,16,768]{2,1,0:T(8,128)(2,1)S(1)}, u32[]{:S(2)}, u32[]{:S(2)}) async-start(bf16[16,16,768]{2,1,0:T(8,128)(2,1)} %bitcast.9), calls=%async_computation.4 | async-start | bytes 786432 | tf_op jit(solution)/shard_map/all_to_all | solution.py:462
  80.4 11.4 %direct.3 = f32[64,768]{1,0:T(8,128)S(1)} custom-call(s32[1024]{0:T(1024)} %own_at.9, s32[1024]{0:T(1024)} %slot_at.9, bf16[384,192,128]{2,1,0:T(8,128)(2,1)} %get-tuple-element.16.tile_ref, bf16[256,768]{1,0:T(8,128)(2,1)S(1)} %bitcast.16), custom_call_target="tpu_custom_call" | custom-call | flops 301989888 | bytes 18874368 | tf_op jit(solution)/shard_map/direct/pallas_call | solution.py:330
  91.9 0.0 copy-done
  91.9 0.7 all-to-all-done.4
  92.6 0.9 %fusion.1 = bf16[64,768]{1,0:T(8,128)(2,1)} fusion(f32[64,768]{1,0:T(8,128)S(1)} %direct.3, bf16[256,768]{1,0:T(8,128)(2,1)S(1)} %bitcast.19, s32[256]{0:T(256)S(1)} %eq.15), kind=kOutput, calls=%fused_computation.5 | convolution fusion | flops 25280512 | bytes 689152 | tf_op jit(solution)/shard_map/dot_general | solution.py:483
Async XLA Ops:
  0.6 18.5 %all-to-all-start = ((s32[16,1,16]{2,1,0:T(1,128)}), s32[16,1,16]{2,1,0:T(1,128)S(1)}, u32[]{:S(2)}, u32[]{:S(2)}) async-start(s32[16,1,16]{2,1,0:T(1,128)} %bitcast.22), calls=%async_computation | async-start | bytes 16384 | tf_op jit(solution)/shard_map/all_to_all | solution.py:462
  18.2 0.9 copy-start.1
  20.3 18.2 %all-to-all-start.1 = ((bf16[16,16,768]{2,1,0:T(8,128)(2,1)}), bf16[16,16,768]{2,1,0:T(8,128)(2,1)S(1)}, u32[]{:S(2)}, u32[]{:S(2)}) async-start(bf16[16,16,768]{2,1,0:T(8,128)(2,1)} %bitcast.3), calls=%async_computation.1 | async-start | bytes 786432 | tf_op jit(solution)/shard_map/all_to_all | solution.py:462
  38.5 17.1 %all-to-all-start.2 = ((bf16[16,16,768]{2,1,0:T(8,128)(2,1)}), bf16[16,16,768]{2,1,0:T(8,128)(2,1)S(1)}, u32[]{:S(2)}, u32[]{:S(2)}) async-start(bf16[16,16,768]{2,1,0:T(8,128)(2,1)} %bitcast.5), calls=%async_computation.2 | async-start | bytes 786432 | tf_op jit(solution)/shard_map/all_to_all | solution.py:462
  55.9 36.0 %copy-start = (bf16[64,768]{1,0:T(8,128)(2,1)}, bf16[64,768]{1,0:T(8,128)(2,1)S(1)}, u32[]{:S(2)}) copy-start(bf16[64,768]{1,0:T(8,128)(2,1)S(1)} %fusion.field_ref) | copy-start | bytes 294916
  57.0 17.5 %all-to-all-start.3 = ((bf16[16,16,768]{2,1,0:T(8,128)(2,1)}), bf16[16,16,768]{2,1,0:T(8,128)(2,1)S(1)}, u32[]{:S(2)}, u32[]{:S(2)}) async-start(bf16[16,16,768]{2,1,0:T(8,128)(2,1)} %bitcast.7), calls=%async_computation.3 | async-start | bytes 786432 | tf_op jit(solution)/shard_map/all_to_all | solution.py:462
  74.4 18.2 %all-to-all-start.4 = ((bf16[16,16,768]{2,1,0:T(8,128)(2,1)}), bf16[16,16,768]{2,1,0:T(8,128)(2,1)S(1)}, u32[]{:S(2)}, u32[]{:S(2)}) async-start(bf16[16,16,768]{2,1,0:T(8,128)(2,1)} %bitcast.9), calls=%async_computation.4 | async-start | bytes 786432 | tf_op jit(solution)/shard_map/all_to_all | solution.py:462

commit v6 on v5

--- a/solution.py
+++ b/solution.py
@@ -111,13 +111,10 @@
 
 def relay_kernel(base, count, final, own_at, slot_at, flag_at, native_ref, field_ref, *rest):
     if final:
-        _, before_at, wide_ref, slot_ref, *rest = rest
-        rest, before_ref = rest[:-1], rest[-1]
+        _, before_ref, wide_ref, slot_ref, *rest = rest
     else:
-        before_at, before_ref = None, None
-        wide_ref, slot_ref, *rest = rest
-    if not final:
-        echo_ref, *rest = rest
+        before_ref = None
+        wide_ref, slot_ref, echo_ref, *rest = rest
     host_ref, guest_ref, made_ref, near_from_ref, line_ref, near_ref, ready, *sums = rest
     unknowns = native_ref.shape[0]
     piece = unknowns // SHARES
@@ -152,9 +149,6 @@
     for n in range(min(2, count)):
         for copy in loads(n):
             copy.start()
-    if final:
-        fetch_before = pltpu.make_async_copy(before_at, before_ref, ready.at[7])
-        fetch_before.start()
     clear(sums)
     fetch_field.wait()
     if not final:
@@ -207,8 +201,6 @@
         if n >= 1:
             store(n - 1).start()
 
-    if final:
-        fetch_before.wait()
     write_slots(sums, slot_ref, before_ref)
     for n in range(max(count - 2, 0), count):
         store(n).wait()
@@ -224,9 +216,12 @@
     stay = pl.BlockSpec(memory_space=pltpu.HBM)
     index = pl.BlockSpec(memory_space=pltpu.SMEM)
     operands = [in_hbm(x) for x in (*indices, native, field)]
+    in_specs = [index] * len(indices) + [stay, stay]
     out_shape = [pltpu.HBM((chunks * PAIRS_PER_CHUNK, depth, LANES), native.dtype)]
     if final:
-        operands += [in_hbm(x) for x in earlier]
+        wide, before = earlier
+        operands += [in_hbm(wide), before]
+        in_specs += [stay, whole]
         out_shape.append(jax.ShapeDtypeStruct((slots, width), jnp.bfloat16))
     else:
         out_shape.append(jax.ShapeDtypeStruct((slots, width), jnp.float32))
@@ -238,14 +233,12 @@
         pltpu.VMEM((fibres, width), field.dtype),
         pltpu.VMEM((2 * unknowns * (LANES + STRIDE_PAD), LANES), jnp.float32),
         pltpu.VMEM((2 * fibres, NRHS, depth), jnp.float32),
-        pltpu.SemaphoreType.DMA((8,)),
+        pltpu.SemaphoreType.DMA((7,)),
     ] + sum_scratch(slots)
-    if final:
-        scratch_shapes.append(pltpu.VMEM((slots, width), jnp.float32))
     return pl.pallas_call(
         functools.partial(relay_kernel, base, count, final),
         out_shape=out_shape,
-        in_specs=[index] * len(indices) + [stay] * (len(operands) - len(indices)),
+        in_specs=in_specs,
         out_specs=[stay] + [whole] * (len(out_shape) - 1),
         scratch_shapes=scratch_shapes,
         input_output_aliases={5: 0} if final else {},

time: 94.3 us -> 93.4 us (level)
  transfers between devices with their start and end apart: 5 -> 5, of which waited for: 3 -> 3; matrix products, arithmetic and copies ran while one was open for 0% -> 0% of each run, Pallas kernels for 60% -> 61%
where the time goes in v6:
time: 93.4 us; the launch traced here: 92.6 us
  Pallas kernels  56.2 us (60%)
  starting transfers between devices  29.5 us (32%)
  matrix products  3.44 us (4%)
  waiting for transfers between devices  2.74 us (3%)
    pallas_call x3, Pallas kernels, product_call(): pl.pallas_call(kernel, out_shape=out_shape, in_specs=[index] * len(indice...  35 us
    all_to_all x5, starting transfers between devices, exchange(): return lax.all_to_all(rows, 'row', 0, 0, tiled=True)  29.5 us
    pallas_call x2, Pallas kernels, relay_mirror(): pl.pallas_call(functools.partial(relay_kernel, base, count, final), out_s...  21.2 us
    all_to_all x5, waiting for transfers between devices, exchange(): return lax.all_to_all(rows, 'row', 0, 0, tiled=True)  2.74 us
    dot_general x2, matrix products, fetch(): rows = jnp.dot(asked_pick, current, preferred_element_type=jnp.float32)  2.19 us
  transfers between devices with their start and end apart: 5, of which 3 were waited for; matrix products, arithmetic and copies ran while one was open for 0% of the time, Pallas kernels for 61%

profile of v6, /device:TPU:0, one launch (start us, length us, event | category | flops | bytes accessed | tf_op | source)
XLA Modules:
  0.0 92.6 jit_solution(7197311994304924298)
XLA Ops:
  0.6 7.4 %all-to-all-start = ((s32[16,1,16]{2,1,0:T(1,128)}), s32[16,1,16]{2,1,0:T(1,128)S(1)}, u32[]{:S(2)}, u32[]{:S(2)}) async-start(s32[16,1,16]{2,1,0:T(1,128)} %bitcast.22), calls=%async_computation | async-start | bytes 16384 | tf_op jit(solution)/shard_map/all_to_all | solution.py:455
  8.0 10.2 %relay.1 = (bf16[384,192,128]{2,1,0:T(8,128)(2,1)}, f32[256,768]{1,0:T(8,128)S(1)}, bf16[64,768]{1,0:T(8,128)(2,1)S(1)}) custom-call(s32[1024]{0:T(1024)} %own_at.9, s32[1024]{0:T(1024)} %slot_at.9, s32[1024]{0:T(1024)} %flag_at.5, bf16[96,96,1024]{2,1,0:T(8,128)(2,1)} %bitcast.17, bf16[64,768]{1,0:T(8,128)(2,1)} %field_ref.3), custom_call_target="tpu_custom_call" | custom-call | flops 603979776 | bytes 18874368 | tf_op jit(solution)/shard_map/relay/pallas_call | solution.py:238
  18.2 0.0 all-to-all-done
  18.2 0.1 eq.15
  18.3 1.1 %convolution_convert_fusion.1 = bf16[256,768]{1,0:T(8,128)(2,1)} fusion(bf16[64,768]{1,0:T(8,128)(2,1)S(1)} %get-tuple-element.18, s32[256]{0:T(256)S(1)} %eq.15), kind=kOutput, calls=%fused_computation.1 | convolution fusion | flops 25378816 | bytes 492544 | tf_op jit(solution)/shard_map/dot_general | solution.py:472
  19.4 6.0 %all-to-all-start.1 = ((bf16[16,16,768]{2,1,0:T(8,128)(2,1)}), bf16[16,16,768]{2,1,0:T(8,128)(2,1)S(1)}, u32[]{:S(2)}, u32[]{:S(2)}) async-start(bf16[16,16,768]{2,1,0:T(8,128)(2,1)} %bitcast.3), calls=%async_computation.1 | async-start | bytes 786432 | tf_op jit(solution)/shard_map/all_to_all | solution.py:455
  25.4 11.0 %relay_rest.1 = (bf16[384,192,128]{2,1,0:T(8,128)(2,1)}, bf16[256,768]{1,0:T(8,128)(2,1)}) custom-call(s32[1024]{0:T(1024)} %own_at.9, s32[1024]{0:T(1024)} %slot_at.9, s32[1024]{0:T(1024)} %flag_at.5, bf16[96,96,1024]{2,1,0:T(8,128)(2,1)} %bitcast.18, bf16[64,768]{1,0:T(8,128)(2,1)} %field_ref.3, ...), custom_call_target="tpu_custom_call", output_to_operand_aliasing={{0}: (5, {})} | custom-call | flops 603979776 | bytes 18874368 | tf_op jit(solution)/shard_map/relay_rest/pallas_call | solution.py:238
  36.4 1.2 %all-to-all-done.1 = bf16[16,16,768]{2,1,0:T(8,128)(2,1)S(1)} async-done(((bf16[16,16,768]{2,1,0:T(8,128)(2,1)}), bf16[16,16,768]{2,1,0:T(8,128)(2,1)S(1)}, u32[]{:S(2)}, u32[]{:S(2)}) %all-to-all-start.1) | async-done | bytes 393248 | tf_op jit(solution)/shard_map/all_to_all | solution.py:455
  37.6 4.8 %all-to-all-start.2 = ((bf16[16,16,768]{2,1,0:T(8,128)(2,1)}), bf16[16,16,768]{2,1,0:T(8,128)(2,1)S(1)}, u32[]{:S(2)}, u32[]{:S(2)}) async-start(bf16[16,16,768]{2,1,0:T(8,128)(2,1)} %bitcast.5), calls=%async_computation.2 | async-start | bytes 786432 | tf_op jit(solution)/shard_map/all_to_all | solution.py:455
  42.4 11.4 %direct.2 = f32[64,768]{1,0:T(8,128)S(1)} custom-call(s32[1024]{0:T(1024)} %own_at.9, s32[1024]{0:T(1024)} %slot_at.9, bf16[384,192,128]{2,1,0:T(8,128)(2,1)} %get-tuple-element.16.tile_ref, bf16[256,768]{1,0:T(8,128)(2,1)S(1)} %bitcast.15), custom_call_target="tpu_custom_call" | custom-call | flops 301989888 | bytes 18874368 | tf_op jit(solution)/shard_map/direct/pallas_call | solution.py:323
  53.9 0.8 all-to-all-done.2
  54.6 0.3 fusion.field_ref
  54.9 0.0 copy-start
  55.0 1.1 %convolution_convert_fusion = bf16[256,768]{1,0:T(8,128)(2,1)} fusion(bf16[64,768]{1,0:T(8,128)(2,1)S(1)} %fusion.field_ref, s32[256]{0:T(256)S(1)} %eq.15), kind=kOutput, calls=%fused_computation | convolution fusion | flops 25378816 | bytes 492544 | tf_op jit(solution)/shard_map/dot_general | solution.py:472
  56.0 5.2 %all-to-all-start.3 = ((bf16[16,16,768]{2,1,0:T(8,128)(2,1)}), bf16[16,16,768]{2,1,0:T(8,128)(2,1)S(1)}, u32[]{:S(2)}, u32[]{:S(2)}) async-start(bf16[16,16,768]{2,1,0:T(8,128)(2,1)} %bitcast.7), calls=%async_computation.3 | async-start | bytes 786432 | tf_op jit(solution)/shard_map/all_to_all | solution.py:455
  61.3 12.2 %mirror.1 = bf16[256,768]{1,0:T(8,128)(2,1)} custom-call(s32[1024]{0:T(1024)} %own_at.9, s32[1024]{0:T(1024)} %slot_at.9, s32[1024]{0:T(1024)} %flag_at.5, bf16[384,192,128]{2,1,0:T(8,128)(2,1)} %get-tuple-element.16.tile_ref, bf16[64,768]{1,0:T(8,128)(2,1)S(1)} %fusion.field_ref), custom_call_target="tpu_custom_call" | custom-call | flops 301989888 | bytes 18874368 | tf_op jit(solution)/shard_map/mirror/pallas_call | solution.py:323
  73.5 0.0 all-to-all-done.3
  73.5 6.0 %all-to-all-start.4 = ((bf16[16,16,768]{2,1,0:T(8,128)(2,1)}), bf16[16,16,768]{2,1,0:T(8,128)(2,1)S(1)}, u32[]{:S(2)}, u32[]{:S(2)}) async-start(bf16[16,16,768]{2,1,0:T(8,128)(2,1)} %bitcast.9), calls=%async_computation.4 | async-start | bytes 786432 | tf_op jit(solution)/shard_map/all_to_all | solution.py:455
  79.5 11.4 %direct.3 = f32[64,768]{1,0:T(8,128)S(1)} custom-call(s32[1024]{0:T(1024)} %own_at.9, s32[1024]{0:T(1024)} %slot_at.9, bf16[384,192,128]{2,1,0:T(8,128)(2,1)} %get-tuple-element.16.tile_ref, bf16[256,768]{1,0:T(8,128)(2,1)S(1)} %bitcast.16), custom_call_target="tpu_custom_call" | custom-call | flops 301989888 | bytes 18874368 | tf_op jit(solution)/shard_map/direct/pallas_call | solution.py:323
  90.9 0.0 copy-done
  90.9 0.8 all-to-all-done.4
  91.7 0.9 %fusion.1 = bf16[64,768]{1,0:T(8,128)(2,1)} fusion(f32[64,768]{1,0:T(8,128)S(1)} %direct.3, bf16[256,768]{1,0:T(8,128)(2,1)S(1)} %bitcast.19, s32[256]{0:T(256)S(1)} %eq.15), kind=kOutput, calls=%fused_computation.5 | convolution fusion | flops 25280512 | bytes 689152 | tf_op jit(solution)/shard_map/dot_general | solution.py:476
Async XLA Ops:
  0.6 17.6 %all-to-all-start = ((s32[16,1,16]{2,1,0:T(1,128)}), s32[16,1,16]{2,1,0:T(1,128)S(1)}, u32[]{:S(2)}, u32[]{:S(2)}) async-start(s32[16,1,16]{2,1,0:T(1,128)} %bitcast.22), calls=%async_computation | async-start | bytes 16384 | tf_op jit(solution)/shard_map/all_to_all | solution.py:455
  19.4 18.2 %all-to-all-start.1 = ((bf16[16,16,768]{2,1,0:T(8,128)(2,1)}), bf16[16,16,768]{2,1,0:T(8,128)(2,1)S(1)}, u32[]{:S(2)}, u32[]{:S(2)}) async-start(bf16[16,16,768]{2,1,0:T(8,128)(2,1)} %bitcast.3), calls=%async_computation.1 | async-start | bytes 786432 | tf_op jit(solution)/shard_map/all_to_all | solution.py:455
  37.6 17.0 %all-to-all-start.2 = ((bf16[16,16,768]{2,1,0:T(8,128)(2,1)}), bf16[16,16,768]{2,1,0:T(8,128)(2,1)S(1)}, u32[]{:S(2)}, u32[]{:S(2)}) async-start(bf16[16,16,768]{2,1,0:T(8,128)(2,1)} %bitcast.5), calls=%async_computation.2 | async-start | bytes 786432 | tf_op jit(solution)/shard_map/all_to_all | solution.py:455
  54.9 36.0 %copy-start = (bf16[64,768]{1,0:T(8,128)(2,1)}, bf16[64,768]{1,0:T(8,128)(2,1)S(1)}, u32[]{:S(2)}) copy-start(bf16[64,768]{1,0:T(8,128)(2,1)S(1)} %fusion.field_ref) | copy-start | bytes 294916
  56.0 17.4 %all-to-all-start.3 = ((bf16[16,16,768]{2,1,0:T(8,128)(2,1)}), bf16[16,16,768]{2,1,0:T(8,128)(2,1)S(1)}, u32[]{:S(2)}, u32[]{:S(2)}) async-start(bf16[16,16,768]{2,1,0:T(8,128)(2,1)} %bitcast.7), calls=%async_computation.3 | async-start | bytes 786432 | tf_op jit(solution)/shard_map/all_to_all | solution.py:455
  73.5 18.2 %all-to-all-start.4 = ((bf16[16,16,768]{2,1,0:T(8,128)(2,1)}), bf16[16,16,768]{2,1,0:T(8,128)(2,1)S(1)}, u32[]{:S(2)}, u32[]{:S(2)}) async-start(bf16[16,16,768]{2,1,0:T(8,128)(2,1)} %bitcast.9), calls=%async_computation.4 | async-start | bytes 786432 | tf_op jit(solution)/shard_map/all_to_all | solution.py:455

commit v7 on v6

--- a/solution.py
+++ b/solution.py
@@ -11,7 +11,7 @@
 LANES = 128
 SHARES = 3
 HOSTS = SHARES + 1
-CHUNKS_HELD = 3
+CHUNKS_HELD = 4
 RELAY_LOOPS = 4
 STRIDE_PAD = 1
 RELAY_VMEM = 52 * 1024 * 1024
@@ -80,7 +80,7 @@
     unknowns = width // NRHS
     piece = unknowns // SHARES
     rows = sums[0].shape[0]
-    step = 32
+    step = 64
 
     def both(pair, at):
         total = pair[0][pl.ds(at, step)] + pair[1][pl.ds(at, step)]

time: 93.4 us -> 92.8 us (level)
  transfers between devices with their start and end apart: 5 -> 5, of which waited for: 3 -> 4; matrix products, arithmetic and copies ran while one was open for 0% -> 0% of each run, Pallas kernels for 61% -> 60%
where the time goes in v7:
time: 92.8 us; the launch traced here: 92 us
  Pallas kernels  55.5 us (60%)
  starting transfers between devices  29 us (31%)
  matrix products  3.44 us (4%)
  waiting for transfers between devices  3.31 us (4%)
    pallas_call x3, Pallas kernels, product_call(): pl.pallas_call(kernel, out_shape=out_shape, in_specs=[index] * len(indice...  34.6 us
    all_to_all x5, starting transfers between devices, exchange(): return lax.all_to_all(rows, 'row', 0, 0, tiled=True)  29 us
    pallas_call x2, Pallas kernels, relay_mirror(): pl.pallas_call(functools.partial(relay_kernel, base, count, final), out_s...  21 us
    all_to_all x5, waiting for transfers between devices, exchange(): return lax.all_to_all(rows, 'row', 0, 0, tiled=True)  3.31 us
    dot_general x2, matrix products, fetch(): rows = jnp.dot(asked_pick, current, preferred_element_type=jnp.float32)  2.19 us
  transfers between devices with their start and end apart: 5, of which 4 were waited for; matrix products, arithmetic and copies ran while one was open for 0% of the time, Pallas kernels for 60%

profile of v7, /device:TPU:0, one launch (start us, length us, event | category | flops | bytes accessed | tf_op | source)
XLA Modules:
  0.0 92.0 jit_solution(7740802978752740538)
XLA Ops:
  0.6 7.4 %all-to-all-start = ((s32[16,1,16]{2,1,0:T(1,128)}), s32[16,1,16]{2,1,0:T(1,128)S(1)}, u32[]{:S(2)}, u32[]{:S(2)}) async-start(s32[16,1,16]{2,1,0:T(1,128)} %bitcast.22), calls=%async_computation | async-start | bytes 16384 | tf_op jit(solution)/shard_map/all_to_all | solution.py:455
  8.0 10.1 %relay.1 = (bf16[384,192,128]{2,1,0:T(8,128)(2,1)}, f32[256,768]{1,0:T(8,128)S(1)}, bf16[64,768]{1,0:T(8,128)(2,1)S(1)}) custom-call(s32[1024]{0:T(1024)} %own_at.9, s32[1024]{0:T(1024)} %slot_at.9, s32[1024]{0:T(1024)} %flag_at.5, bf16[96,96,1024]{2,1,0:T(8,128)(2,1)} %bitcast.17, bf16[64,768]{1,0:T(8,128)(2,1)} %field_ref.3), custom_call_target="tpu_custom_call" | custom-call | flops 603979776 | bytes 18874368 | tf_op jit(solution)/shard_map/relay/pallas_call | solution.py:238
  18.1 0.0 all-to-all-done
  18.1 0.1 eq.15
  18.2 1.1 %convolution_convert_fusion.1 = bf16[256,768]{1,0:T(8,128)(2,1)} fusion(bf16[64,768]{1,0:T(8,128)(2,1)S(1)} %get-tuple-element.18, s32[256]{0:T(256)S(1)} %eq.15), kind=kOutput, calls=%fused_computation.1 | convolution fusion | flops 25378816 | bytes 492544 | tf_op jit(solution)/shard_map/dot_general | solution.py:472
  19.3 6.0 %all-to-all-start.1 = ((bf16[16,16,768]{2,1,0:T(8,128)(2,1)}), bf16[16,16,768]{2,1,0:T(8,128)(2,1)S(1)}, u32[]{:S(2)}, u32[]{:S(2)}) async-start(bf16[16,16,768]{2,1,0:T(8,128)(2,1)} %bitcast.3), calls=%async_computation.1 | async-start | bytes 786432 | tf_op jit(solution)/shard_map/all_to_all | solution.py:455
  25.3 10.9 %relay_rest.1 = (bf16[384,192,128]{2,1,0:T(8,128)(2,1)}, bf16[256,768]{1,0:T(8,128)(2,1)}) custom-call(s32[1024]{0:T(1024)} %own_at.9, s32[1024]{0:T(1024)} %slot_at.9, s32[1024]{0:T(1024)} %flag_at.5, bf16[96,96,1024]{2,1,0:T(8,128)(2,1)} %bitcast.18, bf16[64,768]{1,0:T(8,128)(2,1)} %field_ref.3, ...), custom_call_target="tpu_custom_call", output_to_operand_aliasing={{0}: (5, {})} | custom-call | flops 603979776 | bytes 18874368 | tf_op jit(solution)/shard_map/relay_rest/pallas_call | solution.py:238
  36.2 1.3 %all-to-all-done.1 = bf16[16,16,768]{2,1,0:T(8,128)(2,1)S(1)} async-done(((bf16[16,16,768]{2,1,0:T(8,128)(2,1)}), bf16[16,16,768]{2,1,0:T(8,128)(2,1)S(1)}, u32[]{:S(2)}, u32[]{:S(2)}) %all-to-all-start.1) | async-done | bytes 393248 | tf_op jit(solution)/shard_map/all_to_all | solution.py:455
  37.5 4.7 %all-to-all-start.2 = ((bf16[16,16,768]{2,1,0:T(8,128)(2,1)}), bf16[16,16,768]{2,1,0:T(8,128)(2,1)S(1)}, u32[]{:S(2)}, u32[]{:S(2)}) async-start(bf16[16,16,768]{2,1,0:T(8,128)(2,1)} %bitcast.5), calls=%async_computation.2 | async-start | bytes 786432 | tf_op jit(solution)/shard_map/all_to_all | solution.py:455
  42.2 11.4 %direct.2 = f32[64,768]{1,0:T(8,128)S(1)} custom-call(s32[1024]{0:T(1024)} %own_at.9, s32[1024]{0:T(1024)} %slot_at.9, bf16[384,192,128]{2,1,0:T(8,128)(2,1)} %get-tuple-element.16.tile_ref, bf16[256,768]{1,0:T(8,128)(2,1)S(1)} %bitcast.15), custom_call_target="tpu_custom_call" | custom-call | flops 301989888 | bytes 18874368 | tf_op jit(solution)/shard_map/direct/pallas_call | solution.py:323
  53.7 0.8 all-to-all-done.2
  54.4 0.3 fusion.field_ref
  54.7 0.0 copy-start
  54.7 1.1 %convolution_convert_fusion = bf16[256,768]{1,0:T(8,128)(2,1)} fusion(bf16[64,768]{1,0:T(8,128)(2,1)S(1)} %fusion.field_ref, s32[256]{0:T(256)S(1)} %eq.15), kind=kOutput, calls=%fused_computation | convolution fusion | flops 25378816 | bytes 492544 | tf_op jit(solution)/shard_map/dot_general | solution.py:472
  55.8 5.3 %all-to-all-start.3 = ((bf16[16,16,768]{2,1,0:T(8,128)(2,1)}), bf16[16,16,768]{2,1,0:T(8,128)(2,1)S(1)}, u32[]{:S(2)}, u32[]{:S(2)}) async-start(bf16[16,16,768]{2,1,0:T(8,128)(2,1)} %bitcast.7), calls=%async_computation.3 | async-start | bytes 786432 | tf_op jit(solution)/shard_map/all_to_all | solution.py:455
  61.1 11.7 %mirror.1 = bf16[256,768]{1,0:T(8,128)(2,1)} custom-call(s32[1024]{0:T(1024)} %own_at.9, s32[1024]{0:T(1024)} %slot_at.9, s32[1024]{0:T(1024)} %flag_at.5, bf16[384,192,128]{2,1,0:T(8,128)(2,1)} %get-tuple-element.16.tile_ref, bf16[64,768]{1,0:T(8,128)(2,1)S(1)} %fusion.field_ref), custom_call_target="tpu_custom_call" | custom-call | flops 301989888 | bytes 18874368 | tf_op jit(solution)/shard_map/mirror/pallas_call | solution.py:323
  72.9 0.4 all-to-all-done.3
  73.3 5.6 %all-to-all-start.4 = ((bf16[16,16,768]{2,1,0:T(8,128)(2,1)}), bf16[16,16,768]{2,1,0:T(8,128)(2,1)S(1)}, u32[]{:S(2)}, u32[]{:S(2)}) async-start(bf16[16,16,768]{2,1,0:T(8,128)(2,1)} %bitcast.9), calls=%async_computation.4 | async-start | bytes 786432 | tf_op jit(solution)/shard_map/all_to_all | solution.py:455
  78.9 11.4 %direct.3 = f32[64,768]{1,0:T(8,128)S(1)} custom-call(s32[1024]{0:T(1024)} %own_at.9, s32[1024]{0:T(1024)} %slot_at.9, bf16[384,192,128]{2,1,0:T(8,128)(2,1)} %get-tuple-element.16.tile_ref, bf16[256,768]{1,0:T(8,128)(2,1)S(1)} %bitcast.16), custom_call_target="tpu_custom_call" | custom-call | flops 301989888 | bytes 18874368 | tf_op jit(solution)/shard_map/direct/pallas_call | solution.py:323
  90.3 0.0 copy-done
  90.3 0.8 all-to-all-done.4
  91.1 0.9 %fusion.1 = bf16[64,768]{1,0:T(8,128)(2,1)} fusion(f32[64,768]{1,0:T(8,128)S(1)} %direct.3, bf16[256,768]{1,0:T(8,128)(2,1)S(1)} %bitcast.19, s32[256]{0:T(256)S(1)} %eq.15), kind=kOutput, calls=%fused_computation.5 | convolution fusion | flops 25280512 | bytes 689152 | tf_op jit(solution)/shard_map/dot_general | solution.py:476
Async XLA Ops:
  0.6 17.5 %all-to-all-start = ((s32[16,1,16]{2,1,0:T(1,128)}), s32[16,1,16]{2,1,0:T(1,128)S(1)}, u32[]{:S(2)}, u32[]{:S(2)}) async-start(s32[16,1,16]{2,1,0:T(1,128)} %bitcast.22), calls=%async_computation | async-start | bytes 16384 | tf_op jit(solution)/shard_map/all_to_all | solution.py:455
  19.3 18.2 %all-to-all-start.1 = ((bf16[16,16,768]{2,1,0:T(8,128)(2,1)}), bf16[16,16,768]{2,1,0:T(8,128)(2,1)S(1)}, u32[]{:S(2)}, u32[]{:S(2)}) async-start(bf16[16,16,768]{2,1,0:T(8,128)(2,1)} %bitcast.3), calls=%async_computation.1 | async-start | bytes 786432 | tf_op jit(solution)/shard_map/all_to_all | solution.py:455
  37.5 16.9 %all-to-all-start.2 = ((bf16[16,16,768]{2,1,0:T(8,128)(2,1)}), bf16[16,16,768]{2,1,0:T(8,128)(2,1)S(1)}, u32[]{:S(2)}, u32[]{:S(2)}) async-start(bf16[16,16,768]{2,1,0:T(8,128)(2,1)} %bitcast.5), calls=%async_computation.2 | async-start | bytes 786432 | tf_op jit(solution)/shard_map/all_to_all | solution.py:455
  54.7 35.6 %copy-start = (bf16[64,768]{1,0:T(8,128)(2,1)}, bf16[64,768]{1,0:T(8,128)(2,1)S(1)}, u32[]{:S(2)}) copy-start(bf16[64,768]{1,0:T(8,128)(2,1)S(1)} %fusion.field_ref) | copy-start | bytes 294916
  55.8 17.5 %all-to-all-start.3 = ((bf16[16,16,768]{2,1,0:T(8,128)(2,1)}), bf16[16,16,768]{2,1,0:T(8,128)(2,1)S(1)}, u32[]{:S(2)}, u32[]{:S(2)}) async-start(bf16[16,16,768]{2,1,0:T(8,128)(2,1)} %bitcast.7), calls=%async_computation.3 | async-start | bytes 786432 | tf_op jit(solution)/shard_map/all_to_all | solution.py:455
  73.3 17.8 %all-to-all-start.4 = ((bf16[16,16,768]{2,1,0:T(8,128)(2,1)}), bf16[16,16,768]{2,1,0:T(8,128)(2,1)S(1)}, u32[]{:S(2)}, u32[]{:S(2)}) async-start(bf16[16,16,768]{2,1,0:T(8,128)(2,1)} %bitcast.9), calls=%async_computation.4 | async-start | bytes 786432 | tf_op jit(solution)/shard_map/all_to_all | solution.py:455
